TPU v7x, 32 devices: a whole 2x2x4 slice. The times are simulated.
32 devices in a mesh: grp: 2 (over x), blk: 8 (over z, y), node: 2 (over core).
Axes of the slice: x: 2, y: 2, z: 4, core: 2. Of those that a mesh axis runs over, the one named last changes fastest.
Arguments:
- queries: bfloat16 [32768, 128], P(('grp', 'blk', 'node')), parts along dimension 0, may hold values from -24 to 24
- keys: bfloat16 [32768, 128], P(('grp', 'blk', 'node')), parts along dimension 0, may hold values from -24 to 24
- values: bfloat16 [32768, 128], P(('grp', 'blk', 'node')), parts along dimension 0, may hold values from -6 to 6
- allowed: int32 [256, 128], P('grp'), parts along dimension 0, may hold values from 0 to 1, as said below
Outputs:
- attended: bfloat16 [32768, 128], P(('grp', 'blk', 'node')), parts along dimension 0
There are 2 independent parts, one for each index of `grp`. A program takes and returns all parts, laid end to end along the dimension named above; each array names one. Nothing has to cross between parts.
Inputs may be any that keep to these rules, and one draw needn't show every extreme that they name: allowed[i, i] is 1. allowed[i, j] is 0 where token blocks i and j lie in pairs of 2048 tokens (index // 16) more than 3 apart; in every draw some allowed entries lie exactly 3 pairs apart. Within that range it thins with the frame distance of the blocks.
All inputs are finite; a program needn't handle non-finite values.
Results may differ from a plain program's by a relative error of at most 0.007.
Values may be sent and summed in bfloat16 or wider, within the bound.
No kernel may reach another device: no remote copies, remote signals or barrier semaphores. Data moves between devices by JAX's collectives and lax.ppermute only.
A program may use at most 192 MiB of HBM per device.

v0:
```python
import functools
import math

import jax
import jax.numpy as jnp
from jax import lax
from jax.experimental import pallas as pl
from jax.experimental.pallas import tpu as pltpu
from jax.sharding import PartitionSpec as P

HEAD = 128
BLOCK = 128
FLOOR = -1e30
DROP = -3e38
FACTOR = HEAD ** (-0.5) * math.log2(math.e)
COUNT_AT = 64
WIDE = 4

ANY = pl.BlockSpec(memory_space=pl.ANY)
HBM = pl.BlockSpec(memory_space=pltpu.HBM)
VMEM = pl.BlockSpec(memory_space=pltpu.VMEM)
SMEM = pl.BlockSpec(memory_space=pltpu.SMEM)


def cost(flops, moved, exps=0):
    return pl.CostEstimate(flops=flops, bytes_accessed=moved, transcendentals=exps)


def grant(size):
    return pltpu.CompilerParams(vmem_limit_bytes=size << 20)


def bundle_kernel(k_ref, v_ref, out_ref):
    out_ref[0] = k_ref[...]
    for block in range(v_ref.shape[0] // BLOCK):
        at = pl.ds(block * BLOCK, BLOCK)
        out_ref[1, at, :] = v_ref[at, :].T


def bundle(keys, values):
    rows = keys.shape[0]
    return pl.pallas_call(
        bundle_kernel,
        out_shape=jax.ShapeDtypeStruct((2, rows, HEAD), keys.dtype),
        in_specs=[VMEM, VMEM],
        out_specs=VMEM,
        cost_estimate=cost(0, 4 * rows * HEAD * 2),
        compiler_params=grant(4),
        name="bundle",
    )(keys, values)


def list_kernel(spots, own, allowed_ref, out_ref, rows_ref, sems):
    total = rows_ref.shape[1]
    pos = lax.axis_index("blk")
    core = lax.axis_index("node")
    side = pos % 2
    high = pos // 2
    levels = spots // 2
    mate = pos + 1 - 2 * side
    extra = pos - 1 + 2 * side
    extra_ok = (extra >= 0) & (extra < spots)
    first = high + 1 - 2 * (high % 2)
    second = high - 1 + 2 * (high % 2)
    first_ok = (first >= 0) & (first < levels)
    second_ok = (second >= 0) & (second < levels)
    far = high + 1 - 2 * side
    pair = 2 * own
    query_pairs = (pos, mate, jnp.where(extra_ok, extra, 0))
    copies = []
    for group, who in enumerate(query_pairs):
        begin = pl.multiple_of(who * pair + core * own, own)
        copies.append(
            pltpu.make_async_copy(
                allowed_ref.at[pl.ds(begin, own), :],
                rows_ref.at[pl.ds(group * own, own), :],
                sems.at[group],
            )
        )
    for copy in copies:
        copy.start()
    column = lax.broadcasted_iota(jnp.int32, (own, total), 1)
    inside = column % pair
    place = jnp.where(core == 0, inside, (inside + own) % pair)
    owner = column // pair
    none = jnp.int32(-1)
    one = jnp.where(first_ok, first * 2 + side, none)
    two = jnp.where(second_ok, second * 2 + side, none)
    one_x = jnp.where(first_ok & extra_ok & (first == far), one, none)
    two_x = jnp.where(second_ok & extra_ok & (second == far), two, none)
    near = (owner == pos).astype(jnp.int32)
    beside = ((owner == one) | (owner == two)).astype(jnp.int32)
    beyond = ((owner == one_x) | (owner == two_x)).astype(jnp.int32)
    value = place + jnp.where((owner == two) & (near == 0), pair, 0)
    ahead = (
        lax.broadcasted_iota(jnp.int32, (total, total), 0)
        < lax.broadcasted_iota(jnp.int32, (total, total), 1)
    ).astype(jnp.bfloat16)
    for copy in copies:
        copy.wait()
    lane = lax.broadcasted_iota(jnp.int32, (own, 128), 1)
    jobs = ((0, near, 1), (1, near, 1), (1, beside, 2), (0, beside, 2), (2, beyond, 2))
    for job, (group, wanted, widths) in enumerate(jobs):
        kept = (rows_ref[pl.ds(group * own, own), :] > 0).astype(jnp.int32) * wanted
        rank = lax.dot_general(
            kept.astype(jnp.bfloat16),
            ahead,
            (((1,), (0,)), ((), ())),
            preferred_element_type=jnp.float32,
        ).astype(jnp.int32)
        rank = jnp.where(kept > 0, rank, none)
        count = jnp.sum(kept, axis=1, keepdims=True)
        row = jnp.where(lane == COUNT_AT, count, 0)
        for t in range(widths * pair):
            found = jnp.sum(jnp.where(rank == t, value, 0), axis=1, keepdims=True)
            row = jnp.where(lane == t, found, row)
        out_ref[pl.ds(job * own, own), :] = row


def lists(allowed, own, spots):
    return pl.pallas_call(
        functools.partial(list_kernel, spots, own),
        out_shape=jax.ShapeDtypeStruct((5 * own, 128), jnp.int32),
        in_specs=[ANY],
        out_specs=VMEM,
        scratch_shapes=[
            pltpu.VMEM((3 * own, allowed.shape[1]), jnp.int32),
            pltpu.SemaphoreType.DMA((3,)),
        ],
        cost_estimate=cost(1000, 100000),
        compiler_params=grant(4 + allowed.shape[1] ** 2 // 2**16),
        name="lists",
    )(allowed)


def thirds(value):
    high = value.astype(jnp.bfloat16)
    rest = value - high.astype(jnp.float32)
    middle = rest.astype(jnp.bfloat16)
    low = (rest - middle.astype(jnp.float32)).astype(jnp.bfloat16)
    return high, middle, low


def packed_stats(ref, rows):
    own = rows // BLOCK
    pieces = [ref[pl.ds(rows + n * 2 * own, 2 * own), :].astype(jnp.float32) for n in range(3)]
    both = (pieces[2] + pieces[1]) + pieces[0]
    top, total = both[:own], both[own:]
    return jnp.where(total > 0, top, FLOOR), total


def attend_kernel(job, sources, turn, resume, other, pack, list_ref, q_ref, *refs):
    rows = q_ref.shape[0]
    own = rows // BLOCK
    refs = list(refs)
    take = lambda count: [refs.pop(0) for _ in range(count)]
    source_refs = take(sources)
    if not sources:
        k_ref, v_ref = take(2)
    if resume:
        sum_in, stat_in = take(2)
    if other:
        (other_ref,) = take(1)
    (out_ref,) = take(1)
    if not pack:
        (stat_ref,) = take(1)
        sum_ref = out_ref
    (turned_ref,) = take(1) if turn else (q_ref,)
    if sources:
        k_ref, v_ref = take(2)
    if pack:
        sum_ref, stat_ref = take(2)
    (sems,) = refs
    copies = []
    for n, ref in enumerate(source_refs):
        at = pl.ds(n * rows, rows)
        copies.append(pltpu.make_async_copy(ref.at[0], k_ref.at[at, :], sems.at[2 * n]))
        copies.append(pltpu.make_async_copy(ref.at[1], v_ref.at[at, :], sems.at[2 * n + 1]))
    for copy in copies:
        copy.start()
    counts = [list_ref[job * own + i, COUNT_AT] for i in range(own)]
    steps = counts[0]
    for count in counts[1:]:
        steps = jnp.maximum(steps, count)
    steps = (steps + WIDE - 1) // WIDE
    if resume and other:
        top0, total0 = stat_in[pl.ds(0, own), :], stat_in[pl.ds(own, own), :]
        top1, total1 = packed_stats(other_ref, rows)
        top = jnp.maximum(top0, top1)
        part0 = jnp.exp2((top0 - top) * FACTOR)
        part1 = jnp.exp2((top1 - top) * FACTOR) * total1
        stat_ref[pl.ds(0, own), :] = top
        stat_ref[pl.ds(own, own), :] = part0 * total0 + part1
        for i in range(own):
            mine = pl.ds(i * BLOCK, BLOCK)
            row = slice(i, i + 1)
            theirs = other_ref[mine, :].astype(jnp.float32)
            sum_ref[mine, :] = sum_in[mine, :] * part0[row] + theirs * part1[row]
    elif resume:
        sum_ref[...] = sum_in[...]
        stat_ref[...] = stat_in[...]
    else:
        sum_ref[...] = jnp.zeros_like(sum_ref)
        stat_ref[pl.ds(0, own), :] = jnp.full((own, BLOCK), FLOOR, jnp.float32)
        stat_ref[pl.ds(own, own), :] = jnp.zeros((own, BLOCK), jnp.float32)
    if turn:
        for i in range(own):
            mine = pl.ds(i * BLOCK, BLOCK)
            turned_ref[mine, :] = q_ref[mine, :].T
    for copy in copies:
        copy.wait()
    tops = tuple(stat_ref[pl.ds(i, 1), :] for i in range(own))
    totals = tuple(stat_ref[pl.ds(own + i, 1), :] for i in range(own))

    def step(t, state):
        tops, totals = state
        new_tops, new_totals = [], []
        for i in range(own):
            mine = pl.ds(i * BLOCK, BLOCK)
            turned = turned_ref[mine, :]
            spots, scores, biases = [], [], []
            top = tops[i]
            for u in range(WIDE):
                at = t * WIDE + u
                live = at < counts[i]
                index = jnp.where(live, list_ref[job * own + i, at], 0)
                bias = jnp.where(live, jnp.float32(0.0), jnp.float32(DROP))
                spot = pl.ds(pl.multiple_of(index * BLOCK, BLOCK), BLOCK)
                score = jnp.dot(k_ref[spot, :], turned, preferred_element_type=jnp.float32)
                top = jnp.maximum(top, jnp.max(score, axis=0, keepdims=True) + bias)
                spots.append(spot)
                scores.append(score)
                biases.append(bias)
            fade = jnp.exp2((tops[i] - top) * FACTOR)
            total = totals[i] * fade
            part = None
            for spot, score, bias in zip(spots, scores, biases):
                weight = jnp.exp2((score + (bias - top)) * FACTOR)
                total = total + jnp.sum(weight, axis=0, keepdims=True)
                piece = jnp.dot(
                    v_ref[spot, :],
                    weight.astype(jnp.bfloat16),
                    preferred_element_type=jnp.float32,
                )
                part = piece if part is None else part + piece
            sum_ref[mine, :] = sum_ref[mine, :] * fade + part
            new_tops.append(top)
            new_totals.append(total)
        return tuple(new_tops), tuple(new_totals)

    tops, totals = lax.fori_loop(0, steps, step, (tops, totals))
    stats = jnp.concatenate(tops + totals, axis=0)
    if pack:
        for i in range(own):
            mine = pl.ds(i * BLOCK, BLOCK)
            inverse = 1.0 / jnp.maximum(totals[i], 1e-30)
            out_ref[mine, :] = (sum_ref[mine, :] * inverse).astype(jnp.bfloat16)
        for n, piece in enumerate(thirds(stats)):
            out_ref[pl.ds(rows + n * 2 * own, 2 * own), :] = piece
    else:
        stat_ref[...] = stats


def attend(job, table, queries, sources=(), gathered=(), state=(), other=(), turn=False, pack=False):
    rows = queries.shape[0]
    own = rows // BLOCK
    keys = len(sources) * rows if sources else gathered[0].shape[0]
    square = jax.ShapeDtypeStruct((rows, HEAD), queries.dtype)
    sums = jax.ShapeDtypeStruct((rows, HEAD), jnp.float32)
    stats = jax.ShapeDtypeStruct((2 * own, BLOCK), jnp.float32)
    if pack:
        out_shape = [jax.ShapeDtypeStruct((rows + 6 * own, HEAD), jnp.bfloat16)]
        scratch = [pltpu.VMEM(x.shape, x.dtype) for x in (sums, stats)]
    else:
        out_shape = [sums, stats]
        scratch = []
    if turn:
        out_shape.append(square)
    if sources:
        out_shape += [jax.ShapeDtypeStruct((keys, HEAD), queries.dtype)] * 2
    scratch.append(pltpu.SemaphoreType.DMA((max(1, 2 * len(sources)),)))
    direct = [*gathered, *state, *other]
    return pl.pallas_call(
        functools.partial(attend_kernel, job, len(sources), turn, len(state) > 0, len(other) > 0, pack),
        out_shape=out_shape,
        in_specs=[SMEM, VMEM] + [ANY] * len(sources) + [VMEM] * len(direct),
        out_specs=[VMEM] * len(out_shape),
        scratch_shapes=scratch,
        cost_estimate=cost(1 << 20, 1 << 16),
        compiler_params=grant(8),
        name="attend%d" % job,
    )(table, queries, *sources, *direct)


def merge_kernel(sum_ref, stat_ref, other_ref, out_ref):
    rows = sum_ref.shape[0]
    own = rows // BLOCK
    top0, total0 = stat_ref[pl.ds(0, own), :], stat_ref[pl.ds(own, own), :]
    top1, total1 = packed_stats(other_ref, rows)
    top = jnp.maximum(top0, top1)
    part0 = jnp.exp2((top0 - top) * FACTOR)
    part1 = jnp.exp2((top1 - top) * FACTOR) * total1
    inverse = 1.0 / (part0 * total0 + part1)
    part0, part1 = part0 * inverse, part1 * inverse
    for i in range(own):
        mine = pl.ds(i * BLOCK, BLOCK)
        row = slice(i, i + 1)
        theirs = other_ref[mine, :].astype(jnp.float32)
        mixed = sum_ref[mine, :] * part0[row] + theirs * part1[row]
        out_ref[mine, :] = mixed.astype(jnp.bfloat16).T


def merge(state, other):
    rows = state[0].shape[0]
    return pl.pallas_call(
        merge_kernel,
        out_shape=jax.ShapeDtypeStruct((rows, HEAD), jnp.bfloat16),
        in_specs=[VMEM] * 3,
        out_specs=VMEM,
        cost_estimate=cost(8 * rows * HEAD, 10 * rows * HEAD),
        compiler_params=grant(4),
        name="merge",
    )(*state, other)


def shards(queries, keys, values, allowed):
    rows = queries.shape[0]
    own = rows // BLOCK
    spots = lax.axis_size("blk")
    levels = spots // 2

    def hop(value, target):
        pairs = []
        for i in range(spots):
            high, side = target(i // 2, i % 2)
            if 0 <= high < levels:
                pairs.append((i, high * 2 + side))
        return lax.ppermute(value, "blk", pairs)

    def across(value):
        return hop(value, lambda high, side: (high, 1 - side))

    def swap(value):
        return lax.ppermute(value, "node", [(0, 1), (1, 0)])

    tie = lax.optimization_barrier
    bundled = bundle(keys, values)
    mates = across(queries)
    first = hop(bundled, lambda high, side: (high ^ 1, side))
    second = hop(bundled, lambda high, side: (((high + 1) ^ 1) - 1, side))
    other = swap(bundled)
    table = lists(allowed, own, spots)
    *state, turned, near_k, near_v = attend(0, table, queries, (bundled, other), turn=True)
    near = (near_k, near_v)
    *mate_state, mates = attend(1, table, mates, gathered=near, turn=True)
    first, second, mates, mate_state = tie((first, second, mates, mate_state))
    guests = hop(mates, lambda high, side: (high + 1 - 2 * side, side))
    beside = (first, swap(first), second, swap(second))
    mate_part, *beside = attend(2, table, mates, beside, state=mate_state, pack=True)
    one = across(mate_part)
    (guest_part,) = attend(4, table, guests, gathered=beside, pack=True)
    two = hop(guest_part, lambda high, side: (high - 1 + 2 * side, 1 - side))
    state = attend(3, table, turned, gathered=beside, state=state, other=(one,))
    return merge(state, two)


def solution(mesh):
    placed = (
        P(("grp", "blk", "node"), None),
        P(("grp", "blk", "node"), None),
        P(("grp", "blk", "node"), None),
        P("grp", None),
    )
    return jax.shard_map(
        shards,
        mesh=mesh,
        in_specs=placed,
        out_specs=P(("grp", "blk", "node"), None),
        check_vma=False,
    )
```

profile of v0, /device:TPU:12, one launch (start us, length us, event | category | flops | bytes accessed | tf_op | source)
XLA Modules:
  0.0 43.3 jit_solution(12761753456111558323)
XLA Ops:
  0.0 0.9 %copy-done = bf16[1024,128]{1,0:T(8,128)(2,1)S(1)} copy-done((bf16[1024,128]{1,0:T(8,128)(2,1)S(1)}, bf16[1024,128]{1,0:T(8,128)(2,1)}, u32[]{:S(2)}) %copy-start) | copy-done | bytes 262168
  1.0 0.9 %copy-done.1 = bf16[1024,128]{1,0:T(8,128)(2,1)S(1)} copy-done((bf16[1024,128]{1,0:T(8,128)(2,1)S(1)}, bf16[1024,128]{1,0:T(8,128)(2,1)}, u32[]{:S(2)}) %copy-start.1) | copy-done | bytes 262168
  1.9 0.1 bundle.1.refs_0_
  2.0 0.1 collective-permute-start
  2.1 0.5 %collective-permute-start.1 = (bf16[2,1024,128]{2,1,0:T(8,128)(2,1)S(1)}, bf16[2,1024,128]{2,1,0:T(8,128)(2,1)S(1)}, u32[]{:S(2)}, u32[]{:S(2)}) collective-permute-start(bf16[2,1024,128]{2,1,0:T(8,128)(2,1)S(1)} %bundle.1.refs_0_), channel_id=1, source_target_pairs={{0,4},{2,6},{4,0},{6,2},{8,12},{10,14},{12,8},{14,10},{1,5},{3,7},... | collective-permute-start | bytes 1572872 | tf_op jit(solution)/shard_map/ppermute | solution.py:338
  2.6 4.6 %collective-permute-start.2 = (bf16[2,1024,128]{2,1,0:T(8,128)(2,1)S(1)}, bf16[2,1024,128]{2,1,0:T(8,128)(2,1)S(1)}, u32[]{:S(2)}, u32[]{:S(2)}) collective-permute-start(bf16[2,1024,128]{2,1,0:T(8,128)(2,1)S(1)} %bundle.1.refs_0_), channel_id=1, source_target_pairs={{4,8},{6,10},{8,4},{10,6},{5,9},{7,11},{9,5},{11,7},{20,24},{22,26... | collective-permute-start | bytes 1572872 | tf_op jit(solution)/shard_map/ppermute | solution.py:338
  7.2 0.6 %collective-permute-start.3 = (bf16[1024,128]{1,0:T(8,128)(2,1)S(1)}, bf16[1024,128]{1,0:T(8,128)(2,1)S(1)}, u32[]{:S(2)}, u32[]{:S(2)}) collective-permute-start(bf16[1024,128]{1,0:T(8,128)(2,1)S(1)} %copy-done.2), channel_id=1, source_target_pairs={{0,2},{2,0},{4,6},{6,4},{8,10},{10,8},{12,14},{14,12},{1,3},{3,1},... | collective-permute-start | bytes 786440 | tf_op jit(solution)/shard_map/ppermute | solution.py:338
  7.8 0.5 %lists.1.list_ref = s32[40,128]{1,0:T(8,128)S(1)} custom-call(s32[128,128]{1,0:T(8,128)S(1)} %copy-done.3), custom_call_target="tpu_custom_call" | custom-call | flops 1000 | bytes 100000 | tf_op jit(solution)/shard_map/lists/pallas_call | solution.py:121
  8.4 3.9 %attend0.1 = (f32[1024,128]{1,0:T(8,128)S(1)}, f32[16,128]{1,0:T(8,128)S(1)}, bf16[1024,128]{1,0:T(8,128)(2,1)S(1)}, bf16[2048,128]{1,0:T(8,128)(2,1)S(1)}, bf16[2048,128]{1,0:T(8,128)(2,1)S(1)}) custom-call(s32[40,128]{1,0:T(8,128)S(1)} %lists.1.list_ref, bf16[1024,128]{1,0:T(8,128)(2,1)S(1)} %copy-done.2, bf16[2,1024,128]{2,1,0:T(8,128)(2,1)S(1)} %bundle.1.refs_0_, ...), custom_call_target="tpu_custom_call" | custom-call | flops 1048576 | bytes 65536 | tf_op jit(solution)/shard_map/attend0/pallas_call | solution.py:283
  12.3 3.1 %collective-permute-done.3.q_ref = bf16[1024,128]{1,0:T(8,128)(2,1)S(1)} collective-permute-done((bf16[1024,128]{1,0:T(8,128)(2,1)S(1)}, bf16[1024,128]{1,0:T(8,128)(2,1)S(1)}, u32[]{:S(2)}, u32[]{:S(2)}) %collective-permute-start.3) | collective-permute-done | bytes 262176 | tf_op jit(solution)/shard_map/ppermute | solution.py:338
  15.4 1.9 %attend1.1 = (f32[1024,128]{1,0:T(8,128)S(1)}, f32[16,128]{1,0:T(8,128)S(1)}, bf16[1024,128]{1,0:T(8,128)(2,1)S(1)}) custom-call(s32[40,128]{1,0:T(8,128)S(1)} %lists.1.list_ref, bf16[1024,128]{1,0:T(8,128)(2,1)S(1)} %collective-permute-done.3.q_ref, bf16[2048,128]{1,0:T(8,128)(2,1)S(1)} %get-tuple-element.24.refs_0_, ...), custom_call_target="tpu_custom_call" | custom-call | flops 1048576 | bytes 65536 | tf_op jit(solution)/shard_map/attend1/pallas_call | solution.py:283
  17.4 0.0 collective-permute-done.1.refs_0_
  17.4 2.1 %collective-permute-done.2.refs_2_ = bf16[2,1024,128]{2,1,0:T(8,128)(2,1)S(1)} collective-permute-done((bf16[2,1024,128]{2,1,0:T(8,128)(2,1)S(1)}, bf16[2,1024,128]{2,1,0:T(8,128)(2,1)S(1)}, u32[]{:S(2)}, u32[]{:S(2)}) %collective-permute-start.2) | collective-permute-done | bytes 524320 | tf_op jit(solution)/shard_map/ppermute | solution.py:338
  19.5 0.5 %collective-permute-start.5 = (bf16[2,1024,128]{2,1,0:T(8,128)(2,1)S(1)}, bf16[2,1024,128]{2,1,0:T(8,128)(2,1)S(1)}, u32[]{:S(2)}, u32[]{:S(2)}) collective-permute-start(bf16[2,1024,128]{2,1,0:T(8,128)(2,1)S(1)} %collective-permute-done.2.refs_2_), channel_id=1, source_target_pairs={{0,1},{1,0},{2,3},{3,2},{4,5},{5,4},{6,7},{7,6},{8,9},{9,8},{10,11... | collective-permute-start | bytes 1572872 | tf_op jit(solution)/shard_map/ppermute | solution.py:344
  20.0 1.9 %collective-permute-start.7 = (bf16[1024,128]{1,0:T(8,128)(2,1)S(1)}, bf16[1024,128]{1,0:T(8,128)(2,1)S(1)}, u32[]{:S(2)}, u32[]{:S(2)}) collective-permute-start(bf16[1024,128]{1,0:T(8,128)(2,1)S(1)} %get-tuple-element.29.q_ref), channel_id=1, source_target_pairs={{0,4},{4,8},{6,2},{8,12},{10,6},{14,10},{1,5},{5,9},{7,3},{9,13},{... | collective-permute-start | bytes 786440 | tf_op jit(solution)/shard_map/ppermute | solution.py:338
  21.9 0.2 collective-permute-done.5.refs_3_
  22.1 3.0 %attend2.1 = (bf16[1072,128]{1,0:T(8,128)(2,1)S(1)}, bf16[4096,128]{1,0:T(8,128)(2,1)S(1)}, bf16[4096,128]{1,0:T(8,128)(2,1)S(1)}) custom-call(s32[40,128]{1,0:T(8,128)S(1)} %lists.1.list_ref, bf16[1024,128]{1,0:T(8,128)(2,1)S(1)} %get-tuple-element.29.q_ref, bf16[2,1024,128]{2,1,0:T(8,128)(2,1)S(1)} %collective-permute-done.1.refs_0_, ...), custom_call_target="tpu_custom_call" | custom-call | flops 1048576 | bytes 65536 | tf_op jit(solution)/shard_map/attend2/pallas_call | solution.py:283
  25.2 1.2 %collective-permute-start.6 = (bf16[1072,128]{1,0:T(8,128)(2,1)S(1)}, bf16[1072,128]{1,0:T(8,128)(2,1)S(1)}, u32[]{:S(2)}, u32[]{:S(2)}) collective-permute-start(bf16[1072,128]{1,0:T(8,128)(2,1)S(1)} %get-tuple-element.38), channel_id=1, source_target_pairs={{0,2},{2,0},{4,6},{6,4},{8,10},{10,8},{12,14},{14,12},{1,3},{3,1},... | collective-permute-start | bytes 823304 | tf_op jit(solution)/shard_map/ppermute | solution.py:338
  26.3 3.7 %collective-permute-done.7.q_ref = bf16[1024,128]{1,0:T(8,128)(2,1)S(1)} collective-permute-done((bf16[1024,128]{1,0:T(8,128)(2,1)S(1)}, bf16[1024,128]{1,0:T(8,128)(2,1)S(1)}, u32[]{:S(2)}, u32[]{:S(2)}) %collective-permute-start.7) | collective-permute-done | bytes 262176 | tf_op jit(solution)/shard_map/ppermute | solution.py:338
  30.1 1.9 %attend4.1 = bf16[1072,128]{1,0:T(8,128)(2,1)S(1)} custom-call(s32[40,128]{1,0:T(8,128)S(1)} %lists.1.list_ref, bf16[1024,128]{1,0:T(8,128)(2,1)S(1)} %collective-permute-done.7.q_ref, bf16[4096,128]{1,0:T(8,128)(2,1)S(1)} %get-tuple-element.34.refs_0_, bf16[4096,128]{1,0:T(8,128)(2,1)S(1)} %get-tuple-element.35.refs_1_), custom_call_target="tpu_custom_call" | custom-call | flops 1048576 | bytes 65536 | tf_op jit(solution)/shard_map/attend4/pallas_call | solution.py:283
  32.0 3.6 %collective-permute-start.8 = (bf16[1072,128]{1,0:T(8,128)(2,1)S(1)}, bf16[1072,128]{1,0:T(8,128)(2,1)S(1)}, u32[]{:S(2)}, u32[]{:S(2)}) collective-permute-start(bf16[1072,128]{1,0:T(8,128)(2,1)S(1)} %attend4.1), channel_id=1, source_target_pairs={{2,4},{4,2},{6,8},{8,6},{10,12},{12,10},{3,5},{5,3},{7,9},{9,7},{1... | collective-permute-start | bytes 823304 | tf_op jit(solution)/shard_map/ppermute | solution.py:338
  35.6 1.9 %attend3.1 = (f32[1024,128]{1,0:T(8,128)S(1)}, f32[16,128]{1,0:T(8,128)S(1)}) custom-call(s32[40,128]{1,0:T(8,128)S(1)} %lists.1.list_ref, bf16[1024,128]{1,0:T(8,128)(2,1)S(1)} %get-tuple-element.23.q_ref, bf16[4096,128]{1,0:T(8,128)(2,1)S(1)} %get-tuple-element.34.refs_0_, bf16[4096,128]{1,0:T(8,128)(2,1)S(1)} %get-tuple-element.35.refs_1_, ...), custom_call_target="tpu_custom_call" | custom-call | flops 1048576 | bytes 65536 | tf_op jit(solution)/shard_map/attend3/pallas_call | solution.py:283
  37.5 4.9 %collective-permute-done.8.other_ref = bf16[1072,128]{1,0:T(8,128)(2,1)S(1)} collective-permute-done((bf16[1072,128]{1,0:T(8,128)(2,1)S(1)}, bf16[1072,128]{1,0:T(8,128)(2,1)S(1)}, u32[]{:S(2)}, u32[]{:S(2)}) %collective-permute-start.8) | collective-permute-done | bytes 274464 | tf_op jit(solution)/shard_map/ppermute | solution.py:338
  42.4 0.9 %merge.1 = bf16[1024,128]{1,0:T(8,128)(2,1)} custom-call(f32[1024,128]{1,0:T(8,128)S(1)} %get-tuple-element.39.sum_ref, f32[16,128]{1,0:T(8,128)S(1)} %get-tuple-element.40.stat_ref, bf16[1072,128]{1,0:T(8,128)(2,1)S(1)} %collective-permute-done.8.other_ref), custom_call_target="tpu_custom_call" | custom-call | flops 1048576 | bytes 1310720 | tf_op jit(solution)/shard_map/merge/pallas_call | solution.py:315
  (10 shorter events, 0.0 us)
Async XLA Ops:
  0.0 0.9 %copy-start = (bf16[1024,128]{1,0:T(8,128)(2,1)S(1)}, bf16[1024,128]{1,0:T(8,128)(2,1)}, u32[]{:S(2)}) copy-start(bf16[1024,128]{1,0:T(8,128)(2,1)} %k_ref.1) | copy-start | bytes 786436
  1.0 0.9 %copy-start.1 = (bf16[1024,128]{1,0:T(8,128)(2,1)S(1)}, bf16[1024,128]{1,0:T(8,128)(2,1)}, u32[]{:S(2)}) copy-start(bf16[1024,128]{1,0:T(8,128)(2,1)} %v_ref.1) | copy-start | bytes 786436
  1.9 5.3 %copy-start.2 = (bf16[1024,128]{1,0:T(8,128)(2,1)S(1)}, bf16[1024,128]{1,0:T(8,128)(2,1)}, u32[]{:S(2)}) copy-start(bf16[1024,128]{1,0:T(8,128)(2,1)} %q_ref.1) | copy-start | bytes 786436
  1.9 5.9 %copy-start.3 = (s32[128,128]{1,0:T(8,128)S(1)}, s32[128,128]{1,0:T(8,128)}, u32[]{:S(2)}) copy-start(s32[128,128]{1,0:T(8,128)} %allowed_ref.1) | copy-start | bytes 196612
  2.0 6.3 %collective-permute-start = (bf16[2,1024,128]{2,1,0:T(8,128)(2,1)S(1)}, bf16[2,1024,128]{2,1,0:T(8,128)(2,1)S(1)}, u32[]{:S(2)}, u32[]{:S(2)}) collective-permute-start(bf16[2,1024,128]{2,1,0:T(8,128)(2,1)S(1)} %bundle.1.refs_0_), channel_id=1, source_target_pairs={{0,1},{1,0},{2,3},{3,2},{4,5},{5,4},{6,7},{7,6},{8,9},{9,8},{10,11... | collective-permute-start | bytes 1572872 | tf_op jit(solution)/shard_map/ppermute | solution.py:344
  2.1 15.2 %collective-permute-start.1 = (bf16[2,1024,128]{2,1,0:T(8,128)(2,1)S(1)}, bf16[2,1024,128]{2,1,0:T(8,128)(2,1)S(1)}, u32[]{:S(2)}, u32[]{:S(2)}) collective-permute-start(bf16[2,1024,128]{2,1,0:T(8,128)(2,1)S(1)} %bundle.1.refs_0_), channel_id=1, source_target_pairs={{0,4},{2,6},{4,0},{6,2},{8,12},{10,14},{12,8},{14,10},{1,5},{3,7},... | collective-permute-start | bytes 1572872 | tf_op jit(solution)/shard_map/ppermute | solution.py:338
  2.6 16.8 %collective-permute-start.2 = (bf16[2,1024,128]{2,1,0:T(8,128)(2,1)S(1)}, bf16[2,1024,128]{2,1,0:T(8,128)(2,1)S(1)}, u32[]{:S(2)}, u32[]{:S(2)}) collective-permute-start(bf16[2,1024,128]{2,1,0:T(8,128)(2,1)S(1)} %bundle.1.refs_0_), channel_id=1, source_target_pairs={{4,8},{6,10},{8,4},{10,6},{5,9},{7,11},{9,5},{11,7},{20,24},{22,26... | collective-permute-start | bytes 1572872 | tf_op jit(solution)/shard_map/ppermute | solution.py:338
  7.2 8.2 %collective-permute-start.3 = (bf16[1024,128]{1,0:T(8,128)(2,1)S(1)}, bf16[1024,128]{1,0:T(8,128)(2,1)S(1)}, u32[]{:S(2)}, u32[]{:S(2)}) collective-permute-start(bf16[1024,128]{1,0:T(8,128)(2,1)S(1)} %copy-done.2), channel_id=1, source_target_pairs={{0,2},{2,0},{4,6},{6,4},{8,10},{10,8},{12,14},{14,12},{1,3},{3,1},... | collective-permute-start | bytes 786440 | tf_op jit(solution)/shard_map/ppermute | solution.py:338
  19.5 2.4 %collective-permute-start.4 = (bf16[2,1024,128]{2,1,0:T(8,128)(2,1)S(1)}, bf16[2,1024,128]{2,1,0:T(8,128)(2,1)S(1)}, u32[]{:S(2)}, u32[]{:S(2)}) collective-permute-start(bf16[2,1024,128]{2,1,0:T(8,128)(2,1)S(1)} %collective-permute-done.1.refs_0_), channel_id=1, source_target_pairs={{0,1},{1,0},{2,3},{3,2},{4,5},{5,4},{6,7},{7,6},{8,9},{9,8},{10,11... | collective-permute-start | bytes 1572872 | tf_op jit(solution)/shard_map/ppermute | solution.py:344
  19.5 2.7 %collective-permute-start.5 = (bf16[2,1024,128]{2,1,0:T(8,128)(2,1)S(1)}, bf16[2,1024,128]{2,1,0:T(8,128)(2,1)S(1)}, u32[]{:S(2)}, u32[]{:S(2)}) collective-permute-start(bf16[2,1024,128]{2,1,0:T(8,128)(2,1)S(1)} %collective-permute-done.2.refs_2_), channel_id=1, source_target_pairs={{0,1},{1,0},{2,3},{3,2},{4,5},{5,4},{6,7},{7,6},{8,9},{9,8},{10,11... | collective-permute-start | bytes 1572872 | tf_op jit(solution)/shard_map/ppermute | solution.py:344
  20.0 10.1 %collective-permute-start.7 = (bf16[1024,128]{1,0:T(8,128)(2,1)S(1)}, bf16[1024,128]{1,0:T(8,128)(2,1)S(1)}, u32[]{:S(2)}, u32[]{:S(2)}) collective-permute-start(bf16[1024,128]{1,0:T(8,128)(2,1)S(1)} %get-tuple-element.29.q_ref), channel_id=1, source_target_pairs={{0,4},{4,8},{6,2},{8,12},{10,6},{14,10},{1,5},{5,9},{7,3},{9,13},{... | collective-permute-start | bytes 786440 | tf_op jit(solution)/shard_map/ppermute | solution.py:338
  25.2 10.4 %collective-permute-start.6 = (bf16[1072,128]{1,0:T(8,128)(2,1)S(1)}, bf16[1072,128]{1,0:T(8,128)(2,1)S(1)}, u32[]{:S(2)}, u32[]{:S(2)}) collective-permute-start(bf16[1072,128]{1,0:T(8,128)(2,1)S(1)} %get-tuple-element.38), channel_id=1, source_target_pairs={{0,2},{2,0},{4,6},{6,4},{8,10},{10,8},{12,14},{14,12},{1,3},{3,1},... | collective-permute-start | bytes 823304 | tf_op jit(solution)/shard_map/ppermute | solution.py:338
  32.0 10.4 %collective-permute-start.8 = (bf16[1072,128]{1,0:T(8,128)(2,1)S(1)}, bf16[1072,128]{1,0:T(8,128)(2,1)S(1)}, u32[]{:S(2)}, u32[]{:S(2)}) collective-permute-start(bf16[1072,128]{1,0:T(8,128)(2,1)S(1)} %attend4.1), channel_id=1, source_target_pairs={{2,4},{4,2},{6,8},{8,6},{10,12},{12,10},{3,5},{5,3},{7,9},{9,7},{1... | collective-permute-start | bytes 823304 | tf_op jit(solution)/shard_map/ppermute | solution.py:338
where the time goes:
time: 43.6 us; the launch traced here: 43.3 us
  Pallas kernels  14.2 us (33%)
  waiting for transfers between devices  14.1 us (32%)
  starting transfers between devices  12.9 us (30%)
  local copies, waits for them, and re-layouts  1.91 us (4%)
    ppermute x6, waiting for transfers between devices, hop(): return lax.ppermute(value, 'blk', pairs)  13.8 us
    pallas_call x5, Pallas kernels, attend(): pl.pallas_call(functools.partial(attend_kernel, job, len(sources), turn,...  12.7 us
    ppermute x6, starting transfers between devices, hop(): return lax.ppermute(value, 'blk', pairs)  12.3 us
    unnamed x8, local copies, waits for them, and re-layouts  1.91 us
  transfers between devices with their start and end apart: 9, of which 5 were waited for; matrix products, arithmetic and copies ran while one was open for 0% of the time, Pallas kernels for 31%

commit v1 on v0

--- a/solution.py
+++ b/solution.py
@@ -30,24 +30,46 @@
     return pltpu.CompilerParams(vmem_limit_bytes=size << 20)
 
 
-def bundle_kernel(k_ref, v_ref, out_ref):
-    out_ref[0] = k_ref[...]
-    for block in range(v_ref.shape[0] // BLOCK):
-        at = pl.ds(block * BLOCK, BLOCK)
-        out_ref[1, at, :] = v_ref[at, :].T
-
-
-def bundle(keys, values):
+def bundle_kernel(q_ref, k_ref, v_ref, out_ref, turned_ref, raw_q_ref, raw_v_ref, sems):
+    load_v = pltpu.make_async_copy(v_ref, raw_v_ref, sems.at[0])
+    load_k = pltpu.make_async_copy(k_ref, out_ref.at[0], sems.at[1])
+    load_q = pltpu.make_async_copy(q_ref, raw_q_ref, sems.at[2])
+    load_v.start()
+    load_k.start()
+    load_q.start()
+    blocks = [pl.ds(n * BLOCK, BLOCK) for n in range(raw_v_ref.shape[0] // BLOCK)]
+    load_v.wait()
+    for at in blocks:
+        out_ref[1, at, :] = raw_v_ref[at, :].T
+    load_q.wait()
+    for at in blocks:
+        turned_ref[at, :] = raw_q_ref[at, :].T
+    load_k.wait()
+
+
+def bundle(queries, keys, values):
     rows = keys.shape[0]
+    operands = [
+        pltpu.with_memory_space_constraint(x, pltpu.MemorySpace.HBM)
+        for x in (queries, keys, values)
+    ]
     return pl.pallas_call(
         bundle_kernel,
-        out_shape=jax.ShapeDtypeStruct((2, rows, HEAD), keys.dtype),
-        in_specs=[VMEM, VMEM],
-        out_specs=VMEM,
+        out_shape=(
+            jax.ShapeDtypeStruct((2, rows, HEAD), keys.dtype),
+            jax.ShapeDtypeStruct((rows, HEAD), queries.dtype),
+        ),
+        in_specs=[HBM] * 3,
+        out_specs=[VMEM] * 2,
+        scratch_shapes=[
+            pltpu.VMEM((rows, HEAD), queries.dtype),
+            pltpu.VMEM((rows, HEAD), values.dtype),
+            pltpu.SemaphoreType.DMA((3,)),
+        ],
         cost_estimate=cost(0, 4 * rows * HEAD * 2),
         compiler_params=grant(4),
         name="bundle",
-    )(keys, values)
+    )(*operands)
 
 
 def list_kernel(spots, own, allowed_ref, out_ref, rows_ref, sems):
@@ -91,7 +113,8 @@
     near = (owner == pos).astype(jnp.int32)
     beside = ((owner == one) | (owner == two)).astype(jnp.int32)
     beyond = ((owner == one_x) | (owner == two_x)).astype(jnp.int32)
-    value = place + jnp.where((owner == two) & (near == 0), pair, 0)
+    later = (inside >= own) != (owner == two)
+    value = place + jnp.where(later & (near == 0), pair, 0)
     ahead = (
         lax.broadcasted_iota(jnp.int32, (total, total), 0)
         < lax.broadcasted_iota(jnp.int32, (total, total), 1)
@@ -261,7 +284,7 @@
         stat_ref[...] = stats
 
 
-def attend(job, table, queries, sources=(), gathered=(), state=(), other=(), turn=False, pack=False):
+def attend(job, table, queries, sources=(), gathered=(), state=(), other=(), turn=False, pack=False, spare=0):
     rows = queries.shape[0]
     own = rows // BLOCK
     keys = len(sources) * rows if sources else gathered[0].shape[0]
@@ -269,7 +292,7 @@
     sums = jax.ShapeDtypeStruct((rows, HEAD), jnp.float32)
     stats = jax.ShapeDtypeStruct((2 * own, BLOCK), jnp.float32)
     if pack:
-        out_shape = [jax.ShapeDtypeStruct((rows + 6 * own, HEAD), jnp.bfloat16)]
+        out_shape = [jax.ShapeDtypeStruct((rows + 6 * own + 16 * spare, HEAD), jnp.bfloat16)]
         scratch = [pltpu.VMEM(x.shape, x.dtype) for x in (sums, stats)]
     else:
         out_shape = [sums, stats]
@@ -292,35 +315,40 @@
     )(table, queries, *sources, *direct)
 
 
-def merge_kernel(sum_ref, stat_ref, other_ref, out_ref):
+def merge_kernel(sum_ref, stat_ref, *refs):
+    *other_refs, out_ref = refs
     rows = sum_ref.shape[0]
     own = rows // BLOCK
     top0, total0 = stat_ref[pl.ds(0, own), :], stat_ref[pl.ds(own, own), :]
-    top1, total1 = packed_stats(other_ref, rows)
-    top = jnp.maximum(top0, top1)
-    part0 = jnp.exp2((top0 - top) * FACTOR)
-    part1 = jnp.exp2((top1 - top) * FACTOR) * total1
-    inverse = 1.0 / (part0 * total0 + part1)
-    part0, part1 = part0 * inverse, part1 * inverse
+    others = [packed_stats(ref, rows) for ref in other_refs]
+    top = top0
+    for their_top, _ in others:
+        top = jnp.maximum(top, their_top)
+    share = jnp.exp2((top0 - top) * FACTOR)
+    shares = [jnp.exp2((a - top) * FACTOR) * b for a, b in others]
+    inverse = 1.0 / sum(shares, share * total0)
+    share = share * inverse
+    shares = [x * inverse for x in shares]
     for i in range(own):
         mine = pl.ds(i * BLOCK, BLOCK)
         row = slice(i, i + 1)
-        theirs = other_ref[mine, :].astype(jnp.float32)
-        mixed = sum_ref[mine, :] * part0[row] + theirs * part1[row]
+        mixed = sum_ref[mine, :] * share[row]
+        for ref, part in zip(other_refs, shares):
+            mixed = mixed + ref[mine, :].astype(jnp.float32) * part[row]
         out_ref[mine, :] = mixed.astype(jnp.bfloat16).T
 
 
-def merge(state, other):
+def merge(state, *others):
     rows = state[0].shape[0]
     return pl.pallas_call(
         merge_kernel,
         out_shape=jax.ShapeDtypeStruct((rows, HEAD), jnp.bfloat16),
-        in_specs=[VMEM] * 3,
+        in_specs=[VMEM] * (2 + len(others)),
         out_specs=VMEM,
         cost_estimate=cost(8 * rows * HEAD, 10 * rows * HEAD),
         compiler_params=grant(4),
         name="merge",
-    )(*state, other)
+    )(*state, *others)
 
 
 def shards(queries, keys, values, allowed):
@@ -343,25 +371,52 @@
     def swap(value):
         return lax.ppermute(value, "node", [(0, 1), (1, 0)])
 
+    def trade(value, turn):
+        pairs = []
+        for i in range(spots):
+            high, side = i // 2, i % 2
+            for core in range(2):
+                far = (high ^ 1) if core == turn else ((high + 1) ^ 1) - 1
+                if 0 <= far < levels:
+                    pairs.append((2 * i + core, 2 * (far * 2 + side) + core))
+        return lax.ppermute(value, ("blk", "node"), pairs)
+
+    def visit(value):
+        pairs = []
+        for i in range(spots):
+            high, side = i // 2, i % 2
+            for core in range(2):
+                came = side if core == 0 else 1 - side
+                far = high + 1 - 2 * came
+                if 0 < far < levels - 1:
+                    pairs.append((2 * i + core, 2 * (far * 2 + came) + core))
+        return lax.ppermute(value, ("blk", "node"), pairs)
+
     tie = lax.optimization_barrier
-    bundled = bundle(keys, values)
-    mates = across(queries)
-    first = hop(bundled, lambda high, side: (high ^ 1, side))
-    second = hop(bundled, lambda high, side: (((high + 1) ^ 1) - 1, side))
+    bundled, turned = bundle(queries, keys, values)
+    mates = across(turned)
+    first = trade(bundled, 0)
+    second = trade(bundled, 1)
     other = swap(bundled)
     table = lists(allowed, own, spots)
-    *state, turned, near_k, near_v = attend(0, table, queries, (bundled, other), turn=True)
+    *state, near_k, near_v = attend(0, table, turned, (bundled, other))
     near = (near_k, near_v)
-    *mate_state, mates = attend(1, table, mates, gathered=near, turn=True)
+    mate_state = attend(1, table, mates, gathered=near)
+    core = lax.axis_index("node")
+    parcel = jnp.where(core == 0, mates, turned)
     first, second, mates, mate_state = tie((first, second, mates, mate_state))
-    guests = hop(mates, lambda high, side: (high + 1 - 2 * side, side))
+    guests = visit(parcel)
     beside = (first, swap(first), second, swap(second))
-    mate_part, *beside = attend(2, table, mates, beside, state=mate_state, pack=True)
+    mate_part, *beside = attend(2, table, mates, beside, state=mate_state, pack=True, spare=2)
     one = across(mate_part)
     (guest_part,) = attend(4, table, guests, gathered=beside, pack=True)
-    two = hop(guest_part, lambda high, side: (high - 1 + 2 * side, 1 - side))
-    state = attend(3, table, turned, gathered=beside, state=state, other=(one,))
-    return merge(state, two)
+    homeward = []
+    for i in range(2, spots - 2):
+        high, side = i // 2, i % 2
+        homeward.append((i, (high - 1 + 2 * side) * 2 + 1 - side))
+    two = lax.ppermute(guest_part, "blk", homeward)
+    state = attend(3, table, turned, gathered=beside, state=state)
+    return merge(state, one, two)
 
 
 def solution(mesh):

time: 43.6 us -> 41.5 us (0.952)
  waiting for transfers between devices: 14.1 us -> 7.4 us
  Pallas kernels: 14.2 us -> 18 us
  starting transfers between devices: 12.9 us -> 15.6 us
  local copies, waits for them, and re-layouts: 1.91 us -> 0.01 us
    ppermute x6 -> x2, waiting for transfers between devices: 13.8 us -> 1.18 us  [hop(): return lax.ppermute(value, 'blk', pairs)]
    ppermute x0 -> x4, starting transfers between devices: none -> 12.1 us  [the longest x2 6.97 us: trade(): return lax.ppermute(value, ('blk', 'node'), pairs)]
    ppermute x6 -> x2, starting transfers between devices: 12.3 us -> 2.77 us  [hop(): return lax.ppermute(value, 'blk', pairs)]
    ppermute x0 -> x4, waiting for transfers between devices: none -> 5.27 us  [the longest x1 5.26 us: shards(): two = lax.ppermute(guest_part, 'blk', homeward)]
    pallas_call x5, Pallas kernels: 12.7 us -> 15.3 us  [attend(): pl.pallas_call(functools.partial(attend_kernel, job, len(sources), turn,...]
    unnamed x8 -> x2, local copies, waits for them, and re-layouts: 1.91 us -> 0.01 us
    pallas_call x1, Pallas kernels: 0.12 us -> 1.29 us  [bundle(): pl.pallas_call(bundle_kernel, out_shape=(jax.ShapeDtypeStruct((2, rows, H...]
    ppermute x3, waiting for transfers between devices: 0.23 us -> 0.95 us  [swap(): return lax.ppermute(value, 'node', [(0, 1), (1, 0)])]
  transfers between devices with their start and end apart: 9 -> 9, of which waited for: 5 -> 5; matrix products, arithmetic and copies ran while one was open for 0% -> 0% of each run, Pallas kernels for 31% -> 38%
where the time goes in v1:
time: 41.5 us; the launch traced here: 41.1 us
  Pallas kernels  18 us (43%)
  starting transfers between devices  15.6 us (38%)
  waiting for transfers between devices  7.4 us (18%)
    pallas_call x5, Pallas kernels, attend(): pl.pallas_call(functools.partial(attend_kernel, job, len(sources), turn,...  15.3 us
    ppermute x2, starting transfers between devices, trade(): return lax.ppermute(value, ('blk', 'node'), pairs)  6.97 us
    ppermute x1, waiting for transfers between devices, shards(): two = lax.ppermute(guest_part, 'blk', homeward)  5.26 us
    ppermute x1, starting transfers between devices, shards(): two = lax.ppermute(guest_part, 'blk', homeward)  3.89 us
    ppermute x2, starting transfers between devices, hop(): return lax.ppermute(value, 'blk', pairs)  2.77 us
    ppermute x1, starting transfers between devices, visit(): return lax.ppermute(value, ('blk', 'node'), pairs)  1.29 us
    pallas_call x1, Pallas kernels, bundle(): pl.pallas_call(bundle_kernel, out_shape=(jax.ShapeDtypeStruct((2, rows, H...  1.29 us
    ppermute x2, waiting for transfers between devices, hop(): return lax.ppermute(value, 'blk', pairs)  1.18 us
  transfers between devices with their start and end apart: 9, of which 5 were waited for; matrix products, arithmetic and copies ran while one was open for 0% of the time, Pallas kernels for 38%

profile of v1, /device:TPU:12, one launch (start us, length us, event | category | flops | bytes accessed | tf_op | source)
XLA Modules:
  0.0 41.1 jit_solution(14035097992398921790)
XLA Ops:
  0.0 1.3 %bundle.1 = (bf16[2,1024,128]{2,1,0:T(8,128)(2,1)S(1)}, bf16[1024,128]{1,0:T(8,128)(2,1)S(1)}) custom-call(bf16[1024,128]{1,0:T(8,128)(2,1)} %q_ref.1, bf16[1024,128]{1,0:T(8,128)(2,1)} %k_ref.1, bf16[1024,128]{1,0:T(8,128)(2,1)} %v_ref.1), custom_call_target="tpu_custom_call" | custom-call | bytes 1048576 | tf_op jit(solution)/shard_map/bundle/pallas_call | solution.py:56
  1.3 0.1 collective-permute-start.3
  1.4 2.4 %collective-permute-start = (bf16[2,1024,128]{2,1,0:T(8,128)(2,1)S(1)}, bf16[2,1024,128]{2,1,0:T(8,128)(2,1)S(1)}, u32[]{:S(2)}, u32[]{:S(2)}) collective-permute-start(bf16[2,1024,128]{2,1,0:T(8,128)(2,1)S(1)} %get-tuple-element.24.refs_0_), channel_id=1, source_target_pairs={{0,4},{2,6},{4,0},{5,9},{6,2},{7,11},{8,12},{9,5},{10,14},{11,7},{... | collective-permute-start | bytes 1572872 | tf_op jit(solution)/shard_map/ppermute | solution.py:382
  3.7 4.6 %collective-permute-start.1 = (bf16[2,1024,128]{2,1,0:T(8,128)(2,1)S(1)}, bf16[2,1024,128]{2,1,0:T(8,128)(2,1)S(1)}, u32[]{:S(2)}, u32[]{:S(2)}) collective-permute-start(bf16[2,1024,128]{2,1,0:T(8,128)(2,1)S(1)} %get-tuple-element.24.refs_0_), channel_id=1, source_target_pairs={{1,5},{3,7},{4,8},{5,1},{6,10},{7,3},{8,4},{9,13},{10,6},{11,15},{... | collective-permute-start | bytes 1572872 | tf_op jit(solution)/shard_map/ppermute | solution.py:382
  8.4 0.6 %collective-permute-start.2 = (bf16[1024,128]{1,0:T(8,128)(2,1)S(1)}, bf16[1024,128]{1,0:T(8,128)(2,1)S(1)}, u32[]{:S(2)}, u32[]{:S(2)}) collective-permute-start(bf16[1024,128]{1,0:T(8,128)(2,1)S(1)} %get-tuple-element.23.q_ref), channel_id=1, source_target_pairs={{0,2},{2,0},{4,6},{6,4},{8,10},{10,8},{12,14},{14,12},{1,3},{3,1},... | collective-permute-start | bytes 786440 | tf_op jit(solution)/shard_map/ppermute | solution.py:366
  8.9 0.5 %lists.1.list_ref = s32[40,128]{1,0:T(8,128)S(1)} custom-call(s32[128,128]{1,0:T(8,128)S(1)} %copy-done), custom_call_target="tpu_custom_call" | custom-call | flops 1000 | bytes 100000 | tf_op jit(solution)/shard_map/lists/pallas_call | solution.py:144
  9.5 0.0 collective-permute-done.3.refs_1_
  9.5 4.7 %attend0.1 = (f32[1024,128]{1,0:T(8,128)S(1)}, f32[16,128]{1,0:T(8,128)S(1)}, bf16[2048,128]{1,0:T(8,128)(2,1)S(1)}, bf16[2048,128]{1,0:T(8,128)(2,1)S(1)}) custom-call(s32[40,128]{1,0:T(8,128)S(1)} %lists.1.list_ref, bf16[1024,128]{1,0:T(8,128)(2,1)S(1)} %get-tuple-element.23.q_ref, bf16[2,1024,128]{2,1,0:T(8,128)(2,1)S(1)} %get-tuple-element.24.refs_0_, ...), custom_call_target="tpu_custom_call" | custom-call | flops 1048576 | bytes 65536 | tf_op jit(solution)/shard_map/attend0/pallas_call | solution.py:306
  14.2 1.0 %collective-permute-done.2.q_ref = bf16[1024,128]{1,0:T(8,128)(2,1)S(1)} collective-permute-done((bf16[1024,128]{1,0:T(8,128)(2,1)S(1)}, bf16[1024,128]{1,0:T(8,128)(2,1)S(1)}, u32[]{:S(2)}, u32[]{:S(2)}) %collective-permute-start.2) | collective-permute-done | bytes 262176 | tf_op jit(solution)/shard_map/ppermute | solution.py:366
  15.3 2.8 %attend1.1 = (f32[1024,128]{1,0:T(8,128)S(1)}, f32[16,128]{1,0:T(8,128)S(1)}) custom-call(s32[40,128]{1,0:T(8,128)S(1)} %lists.1.list_ref, bf16[1024,128]{1,0:T(8,128)(2,1)S(1)} %collective-permute-done.2.q_ref, bf16[2048,128]{1,0:T(8,128)(2,1)S(1)} %get-tuple-element.25.refs_0_, bf16[2048,128]{1,0:T(8,128)(2,1)S(1)} %get-tuple-element.26.refs_1_), custom_call_target="tpu_custom_call" | custom-call | flops 1048576 | bytes 65536 | tf_op jit(solution)/shard_map/attend1/pallas_call | solution.py:306
  18.1 0.0 collective-permute-done.1.refs_2_
  18.1 0.1 collective-permute-start.4
  18.2 0.5 %collective-permute-start.5 = (bf16[2,1024,128]{2,1,0:T(8,128)(2,1)S(1)}, bf16[2,1024,128]{2,1,0:T(8,128)(2,1)}, u32[]{:S(2)}, u32[]{:S(2)}) collective-permute-start(bf16[2,1024,128]{2,1,0:T(8,128)(2,1)S(1)} %collective-permute-done.1.refs_2_), channel_id=1, source_target_pairs={{0,1},{1,0},{2,3},{3,2},{4,5},{5,4},{6,7},{7,6},{8,9},{9,8},{10,11... | collective-permute-start | bytes 1572872 | tf_op jit(solution)/shard_map/ppermute | solution.py:372
  18.7 1.3 %collective-permute-start.7 = (bf16[1024,128]{1,0:T(8,128)(2,1)S(1)}, bf16[1024,128]{1,0:T(8,128)(2,1)S(1)}, u32[]{:S(2)}, u32[]{:S(2)}) collective-permute-start(bf16[1024,128]{1,0:T(8,128)(2,1)S(1)} %broadcast_select_fusion), channel_id=1, source_target_pairs={{0,4},{3,5},{4,8},{7,9},{9,7},{10,6},{13,11},{14,10},{16,20},{19,2... | collective-permute-start | bytes 786440 | tf_op jit(solution)/shard_map/ppermute | solution.py:393
  20.0 0.1 collective-permute-done.4.refs_1_
  20.1 0.9 %collective-permute-done.5.refs_3_ = bf16[2,1024,128]{2,1,0:T(8,128)(2,1)} collective-permute-done((bf16[2,1024,128]{2,1,0:T(8,128)(2,1)S(1)}, bf16[2,1024,128]{2,1,0:T(8,128)(2,1)}, u32[]{:S(2)}, u32[]{:S(2)}) %collective-permute-start.5) | collective-permute-done | bytes 524320 | tf_op jit(solution)/shard_map/ppermute | solution.py:372
  20.9 4.0 %attend2.1 = (bf16[1104,128]{1,0:T(8,128)(2,1)S(1)}, bf16[4096,128]{1,0:T(8,128)(2,1)S(1)}, bf16[4096,128]{1,0:T(8,128)(2,1)S(1)}) custom-call(s32[40,128]{1,0:T(8,128)S(1)} %lists.1.list_ref, bf16[1024,128]{1,0:T(8,128)(2,1)S(1)} %collective-permute-done.2.q_ref, bf16[2,1024,128]{2,1,0:T(8,128)(2,1)S(1)} %collective-permute-done.refs_0_, ...), custom_call_target="tpu_custom_call" | custom-call | flops 1048576 | bytes 65536 | tf_op jit(solution)/shard_map/attend2/pallas_call | solution.py:306
  24.9 2.2 %collective-permute-start.6 = (bf16[1104,128]{1,0:T(8,128)(2,1)S(1)}, bf16[1104,128]{1,0:T(8,128)(2,1)S(1)}, u32[]{:S(2)}, u32[]{:S(2)}) collective-permute-start(bf16[1104,128]{1,0:T(8,128)(2,1)S(1)} %get-tuple-element.40), channel_id=1, source_target_pairs={{0,2},{2,0},{4,6},{6,4},{8,10},{10,8},{12,14},{14,12},{1,3},{3,1},... | collective-permute-start | bytes 847880 | tf_op jit(solution)/shard_map/ppermute | solution.py:366
  27.1 1.9 %attend4.1 = bf16[1072,128]{1,0:T(8,128)(2,1)S(1)} custom-call(s32[40,128]{1,0:T(8,128)S(1)} %lists.1.list_ref, bf16[1024,128]{1,0:T(8,128)(2,1)S(1)} %collective-permute-done.7.q_ref, bf16[4096,128]{1,0:T(8,128)(2,1)S(1)} %get-tuple-element.34.refs_0_, bf16[4096,128]{1,0:T(8,128)(2,1)S(1)} %get-tuple-element.35.refs_1_), custom_call_target="tpu_custom_call" | custom-call | flops 1048576 | bytes 65536 | tf_op jit(solution)/shard_map/attend4/pallas_call | solution.py:306
  29.0 3.9 %collective-permute-start.8 = (bf16[1072,128]{1,0:T(8,128)(2,1)S(1)}, bf16[1072,128]{1,0:T(8,128)(2,1)S(1)}, u32[]{:S(2)}, u32[]{:S(2)}) collective-permute-start(bf16[1072,128]{1,0:T(8,128)(2,1)S(1)} %attend4.1), channel_id=1, source_target_pairs={{4,2},{6,8},{8,6},{10,12},{5,3},{7,9},{9,7},{11,13},{20,18},{22,24... | collective-permute-start | bytes 823304 | tf_op jit(solution)/shard_map/ppermute | solution.py:417
  32.9 1.9 %attend3.1 = (f32[1024,128]{1,0:T(8,128)S(1)}, f32[16,128]{1,0:T(8,128)S(1)}) custom-call(s32[40,128]{1,0:T(8,128)S(1)} %lists.1.list_ref, bf16[1024,128]{1,0:T(8,128)(2,1)S(1)} %get-tuple-element.23.q_ref, bf16[4096,128]{1,0:T(8,128)(2,1)S(1)} %get-tuple-element.34.refs_0_, bf16[4096,128]{1,0:T(8,128)(2,1)S(1)} %get-tuple-element.35.refs_1_, ...), custom_call_target="tpu_custom_call" | custom-call | flops 1048576 | bytes 65536 | tf_op jit(solution)/shard_map/attend3/pallas_call | solution.py:306
  34.8 5.3 %collective-permute-done.8.refs_1_ = bf16[1072,128]{1,0:T(8,128)(2,1)S(1)} collective-permute-done((bf16[1072,128]{1,0:T(8,128)(2,1)S(1)}, bf16[1072,128]{1,0:T(8,128)(2,1)S(1)}, u32[]{:S(2)}, u32[]{:S(2)}) %collective-permute-start.8) | collective-permute-done | bytes 274464 | tf_op jit(solution)/shard_map/ppermute | solution.py:417
  40.1 0.1 collective-permute-done.6.refs_0_
  40.2 0.9 %merge.1 = bf16[1024,128]{1,0:T(8,128)(2,1)} custom-call(f32[1024,128]{1,0:T(8,128)S(1)} %get-tuple-element.38.sum_ref, f32[16,128]{1,0:T(8,128)S(1)} %get-tuple-element.39.stat_ref, bf16[1104,128]{1,0:T(8,128)(2,1)S(1)} %collective-permute-done.6.refs_0_, bf16[1072,128]{1,0:T(8,128)(2,1)S(1)} %collective-permute-done.8.refs_1_), custom_call_target="tpu_custom_call" | custom-call | flops 1048576 | bytes 1310720 | tf_op jit(solution)/shard_map/merge/pallas_call | solution.py:343
  (5 shorter events, 0.0 us)
Async XLA Ops:
  0.0 8.9 %copy-start = (s32[128,128]{1,0:T(8,128)S(1)}, s32[128,128]{1,0:T(8,128)}, u32[]{:S(2)}) copy-start(s32[128,128]{1,0:T(8,128)} %allowed_ref.1) | copy-start | bytes 196612
  1.3 8.2 %collective-permute-start.3 = (bf16[2,1024,128]{2,1,0:T(8,128)(2,1)S(1)}, bf16[2,1024,128]{2,1,0:T(8,128)(2,1)S(1)}, u32[]{:S(2)}, u32[]{:S(2)}) collective-permute-start(bf16[2,1024,128]{2,1,0:T(8,128)(2,1)S(1)} %get-tuple-element.24.refs_0_), channel_id=1, source_target_pairs={{0,1},{1,0},{2,3},{3,2},{4,5},{5,4},{6,7},{7,6},{8,9},{9,8},{10,11... | collective-permute-start | bytes 1572872 | tf_op jit(solution)/shard_map/ppermute | solution.py:372
  1.4 16.7 %collective-permute-start = (bf16[2,1024,128]{2,1,0:T(8,128)(2,1)S(1)}, bf16[2,1024,128]{2,1,0:T(8,128)(2,1)S(1)}, u32[]{:S(2)}, u32[]{:S(2)}) collective-permute-start(bf16[2,1024,128]{2,1,0:T(8,128)(2,1)S(1)} %get-tuple-element.24.refs_0_), channel_id=1, source_target_pairs={{0,4},{2,6},{4,0},{5,9},{6,2},{7,11},{8,12},{9,5},{10,14},{11,7},{... | collective-permute-start | bytes 1572872 | tf_op jit(solution)/shard_map/ppermute | solution.py:382
  3.7 14.3 %collective-permute-start.1 = (bf16[2,1024,128]{2,1,0:T(8,128)(2,1)S(1)}, bf16[2,1024,128]{2,1,0:T(8,128)(2,1)S(1)}, u32[]{:S(2)}, u32[]{:S(2)}) collective-permute-start(bf16[2,1024,128]{2,1,0:T(8,128)(2,1)S(1)} %get-tuple-element.24.refs_0_), channel_id=1, source_target_pairs={{1,5},{3,7},{4,8},{5,1},{6,10},{7,3},{8,4},{9,13},{10,6},{11,15},{... | collective-permute-start | bytes 1572872 | tf_op jit(solution)/shard_map/ppermute | solution.py:382
  8.4 6.9 %collective-permute-start.2 = (bf16[1024,128]{1,0:T(8,128)(2,1)S(1)}, bf16[1024,128]{1,0:T(8,128)(2,1)S(1)}, u32[]{:S(2)}, u32[]{:S(2)}) collective-permute-start(bf16[1024,128]{1,0:T(8,128)(2,1)S(1)} %get-tuple-element.23.q_ref), channel_id=1, source_target_pairs={{0,2},{2,0},{4,6},{6,4},{8,10},{10,8},{12,14},{14,12},{1,3},{3,1},... | collective-permute-start | bytes 786440 | tf_op jit(solution)/shard_map/ppermute | solution.py:366
  18.1 2.0 %collective-permute-start.4 = (bf16[2,1024,128]{2,1,0:T(8,128)(2,1)S(1)}, bf16[2,1024,128]{2,1,0:T(8,128)(2,1)S(1)}, u32[]{:S(2)}, u32[]{:S(2)}) collective-permute-start(bf16[2,1024,128]{2,1,0:T(8,128)(2,1)S(1)} %collective-permute-done.refs_0_), channel_id=1, source_target_pairs={{0,1},{1,0},{2,3},{3,2},{4,5},{5,4},{6,7},{7,6},{8,9},{9,8},{10,11... | collective-permute-start | bytes 1572872 | tf_op jit(solution)/shard_map/ppermute | solution.py:372
  18.2 2.8 %collective-permute-start.5 = (bf16[2,1024,128]{2,1,0:T(8,128)(2,1)S(1)}, bf16[2,1024,128]{2,1,0:T(8,128)(2,1)}, u32[]{:S(2)}, u32[]{:S(2)}) collective-permute-start(bf16[2,1024,128]{2,1,0:T(8,128)(2,1)S(1)} %collective-permute-done.1.refs_2_), channel_id=1, source_target_pairs={{0,1},{1,0},{2,3},{3,2},{4,5},{5,4},{6,7},{7,6},{8,9},{9,8},{10,11... | collective-permute-start | bytes 1572872 | tf_op jit(solution)/shard_map/ppermute | solution.py:372
  18.7 8.4 %collective-permute-start.7 = (bf16[1024,128]{1,0:T(8,128)(2,1)S(1)}, bf16[1024,128]{1,0:T(8,128)(2,1)S(1)}, u32[]{:S(2)}, u32[]{:S(2)}) collective-permute-start(bf16[1024,128]{1,0:T(8,128)(2,1)S(1)} %broadcast_select_fusion), channel_id=1, source_target_pairs={{0,4},{3,5},{4,8},{7,9},{9,7},{10,6},{13,11},{14,10},{16,20},{19,2... | collective-permute-start | bytes 786440 | tf_op jit(solution)/shard_map/ppermute | solution.py:393
  24.9 15.3 %collective-permute-start.6 = (bf16[1104,128]{1,0:T(8,128)(2,1)S(1)}, bf16[1104,128]{1,0:T(8,128)(2,1)S(1)}, u32[]{:S(2)}, u32[]{:S(2)}) collective-permute-start(bf16[1104,128]{1,0:T(8,128)(2,1)S(1)} %get-tuple-element.40), channel_id=1, source_target_pairs={{0,2},{2,0},{4,6},{6,4},{8,10},{10,8},{12,14},{14,12},{1,3},{3,1},... | collective-permute-start | bytes 847880 | tf_op jit(solution)/shard_map/ppermute | solution.py:366
  29.0 11.0 %collective-permute-start.8 = (bf16[1072,128]{1,0:T(8,128)(2,1)S(1)}, bf16[1072,128]{1,0:T(8,128)(2,1)S(1)}, u32[]{:S(2)}, u32[]{:S(2)}) collective-permute-start(bf16[1072,128]{1,0:T(8,128)(2,1)S(1)} %attend4.1), channel_id=1, source_target_pairs={{4,2},{6,8},{8,6},{10,12},{5,3},{7,9},{9,7},{11,13},{20,18},{22,24... | collective-permute-start | bytes 823304 | tf_op jit(solution)/shard_map/ppermute | solution.py:417

commit v2 on v1

--- a/solution.py
+++ b/solution.py
@@ -172,7 +172,7 @@
     return jnp.where(total > 0, top, FLOOR), total
 
 
-def attend_kernel(job, sources, turn, resume, other, pack, list_ref, q_ref, *refs):
+def attend_kernel(base, sources, resume, pack, list_ref, q_ref, *refs):
     rows = q_ref.shape[0]
     own = rows // BLOCK
     refs = list(refs)
@@ -181,19 +181,12 @@
     if not sources:
         k_ref, v_ref = take(2)
     if resume:
-        sum_in, stat_in = take(2)
-    if other:
-        (other_ref,) = take(1)
-    (out_ref,) = take(1)
-    if not pack:
-        (stat_ref,) = take(1)
-        sum_ref = out_ref
-    (turned_ref,) = take(1) if turn else (q_ref,)
+        take(2)
+    if pack:
+        (out_ref,) = take(1)
     if sources:
         k_ref, v_ref = take(2)
-    if pack:
-        sum_ref, stat_ref = take(2)
-    (sems,) = refs
+    sum_ref, stat_ref, sems = refs
     copies = []
     for n, ref in enumerate(source_refs):
         at = pl.ds(n * rows, rows)
@@ -201,35 +194,15 @@
         copies.append(pltpu.make_async_copy(ref.at[1], v_ref.at[at, :], sems.at[2 * n + 1]))
     for copy in copies:
         copy.start()
-    counts = [list_ref[job * own + i, COUNT_AT] for i in range(own)]
+    counts = [list_ref[base + i, COUNT_AT] for i in range(own)]
     steps = counts[0]
     for count in counts[1:]:
         steps = jnp.maximum(steps, count)
     steps = (steps + WIDE - 1) // WIDE
-    if resume and other:
-        top0, total0 = stat_in[pl.ds(0, own), :], stat_in[pl.ds(own, own), :]
-        top1, total1 = packed_stats(other_ref, rows)
-        top = jnp.maximum(top0, top1)
-        part0 = jnp.exp2((top0 - top) * FACTOR)
-        part1 = jnp.exp2((top1 - top) * FACTOR) * total1
-        stat_ref[pl.ds(0, own), :] = top
-        stat_ref[pl.ds(own, own), :] = part0 * total0 + part1
-        for i in range(own):
-            mine = pl.ds(i * BLOCK, BLOCK)
-            row = slice(i, i + 1)
-            theirs = other_ref[mine, :].astype(jnp.float32)
-            sum_ref[mine, :] = sum_in[mine, :] * part0[row] + theirs * part1[row]
-    elif resume:
-        sum_ref[...] = sum_in[...]
-        stat_ref[...] = stat_in[...]
-    else:
+    if not resume:
         sum_ref[...] = jnp.zeros_like(sum_ref)
         stat_ref[pl.ds(0, own), :] = jnp.full((own, BLOCK), FLOOR, jnp.float32)
         stat_ref[pl.ds(own, own), :] = jnp.zeros((own, BLOCK), jnp.float32)
-    if turn:
-        for i in range(own):
-            mine = pl.ds(i * BLOCK, BLOCK)
-            turned_ref[mine, :] = q_ref[mine, :].T
     for copy in copies:
         copy.wait()
     tops = tuple(stat_ref[pl.ds(i, 1), :] for i in range(own))
@@ -240,13 +213,13 @@
         new_tops, new_totals = [], []
         for i in range(own):
             mine = pl.ds(i * BLOCK, BLOCK)
-            turned = turned_ref[mine, :]
+            turned = q_ref[mine, :]
             spots, scores, biases = [], [], []
             top = tops[i]
             for u in range(WIDE):
                 at = t * WIDE + u
                 live = at < counts[i]
-                index = jnp.where(live, list_ref[job * own + i, at], 0)
+                index = jnp.where(live, list_ref[base + i, at], 0)
                 bias = jnp.where(live, jnp.float32(0.0), jnp.float32(DROP))
                 spot = pl.ds(pl.multiple_of(index * BLOCK, BLOCK), BLOCK)
                 score = jnp.dot(k_ref[spot, :], turned, preferred_element_type=jnp.float32)
@@ -255,8 +228,7 @@
                 scores.append(score)
                 biases.append(bias)
             fade = jnp.exp2((tops[i] - top) * FACTOR)
-            total = totals[i] * fade
-            part = None
+            total, part = totals[i] * fade, None
             for spot, score, bias in zip(spots, scores, biases):
                 weight = jnp.exp2((score + (bias - top)) * FACTOR)
                 total = total + jnp.sum(weight, axis=0, keepdims=True)
@@ -273,46 +245,78 @@
 
     tops, totals = lax.fori_loop(0, steps, step, (tops, totals))
     stats = jnp.concatenate(tops + totals, axis=0)
-    if pack:
+    if not pack:
+        stat_ref[...] = stats
+    else:
         for i in range(own):
             mine = pl.ds(i * BLOCK, BLOCK)
             inverse = 1.0 / jnp.maximum(totals[i], 1e-30)
             out_ref[mine, :] = (sum_ref[mine, :] * inverse).astype(jnp.bfloat16)
         for n, piece in enumerate(thirds(stats)):
             out_ref[pl.ds(rows + n * 2 * own, 2 * own), :] = piece
-    else:
-        stat_ref[...] = stats
-
-
-def attend(job, table, queries, sources=(), gathered=(), state=(), other=(), turn=False, pack=False, spare=0):
+        spare = out_ref.shape[0] - rows - 6 * own
+        if spare:
+            out_ref[pl.ds(rows + 6 * own, spare), :] = jnp.zeros((spare, HEAD), out_ref.dtype)
+
+
+def attend(job, table, queries, sources=(), gathered=(), state=(), pack=False, spare=0):
     rows = queries.shape[0]
     own = rows // BLOCK
     keys = len(sources) * rows if sources else gathered[0].shape[0]
-    square = jax.ShapeDtypeStruct((rows, HEAD), queries.dtype)
-    sums = jax.ShapeDtypeStruct((rows, HEAD), jnp.float32)
-    stats = jax.ShapeDtypeStruct((2 * own, BLOCK), jnp.float32)
+    out_shape = []
     if pack:
-        out_shape = [jax.ShapeDtypeStruct((rows + 6 * own + 16 * spare, HEAD), jnp.bfloat16)]
-        scratch = [pltpu.VMEM(x.shape, x.dtype) for x in (sums, stats)]
-    else:
-        out_shape = [sums, stats]
-        scratch = []
-    if turn:
-        out_shape.append(square)
+        height = rows + 6 * own + 16 * spare
+        out_shape.append(jax.ShapeDtypeStruct((height, HEAD), jnp.bfloat16))
     if sources:
         out_shape += [jax.ShapeDtypeStruct((keys, HEAD), queries.dtype)] * 2
-    scratch.append(pltpu.SemaphoreType.DMA((max(1, 2 * len(sources)),)))
-    direct = [*gathered, *state, *other]
+    kept = [
+        jax.ShapeDtypeStruct((rows, HEAD), jnp.float32),
+        jax.ShapeDtypeStruct((2 * own, BLOCK), jnp.float32),
+    ]
+    scratch = []
+    if pack and not state:
+        scratch = [pltpu.VMEM(x.shape, x.dtype) for x in kept]
+    else:
+        out_shape += kept
+    direct = [*gathered, *state]
+    operands = 2 + len(sources) + len(direct)
+    outs = len(out_shape)
+    aliases = {operands - 2: outs - 2, operands - 1: outs - 1} if state else {}
     return pl.pallas_call(
-        functools.partial(attend_kernel, job, len(sources), turn, len(state) > 0, len(other) > 0, pack),
+        functools.partial(attend_kernel, job * own, len(sources), len(state) > 0, pack),
         out_shape=out_shape,
         in_specs=[SMEM, VMEM] + [ANY] * len(sources) + [VMEM] * len(direct),
-        out_specs=[VMEM] * len(out_shape),
-        scratch_shapes=scratch,
+        out_specs=[VMEM] * outs,
+        scratch_shapes=scratch + [pltpu.SemaphoreType.DMA((max(1, 2 * len(sources)),))],
+        input_output_aliases=aliases,
         cost_estimate=cost(1 << 20, 1 << 16),
         compiler_params=grant(8),
         name="attend%d" % job,
     )(table, queries, *sources, *direct)
+
+
+def choose_kernel(one_ref, two_ref, out_ref):
+    core = lax.axis_index("node")
+
+    @pl.when(core == 0)
+    def _():
+        out_ref[...] = one_ref[...]
+
+    @pl.when(core != 0)
+    def _():
+        out_ref[...] = two_ref[...]
+
+
+def choose(one, two):
+    return pl.pallas_call(
+        choose_kernel,
+        out_shape=jax.ShapeDtypeStruct(one.shape, one.dtype),
+        in_specs=[VMEM] * 2,
+        out_specs=VMEM,
+        cost_estimate=cost(1 << 10, 1 << 10),
+        compiler_params=grant(1),
+        name="choose",
+    )(one, two)
 
 
 def merge_kernel(sum_ref, stat_ref, *refs):
@@ -399,23 +403,21 @@
     second = trade(bundled, 1)
     other = swap(bundled)
     table = lists(allowed, own, spots)
-    *state, near_k, near_v = attend(0, table, turned, (bundled, other))
-    near = (near_k, near_v)
+    *near, sums, stats = attend(0, table, turned, (bundled, other))
     mate_state = attend(1, table, mates, gathered=near)
-    core = lax.axis_index("node")
-    parcel = jnp.where(core == 0, mates, turned)
+    parcel = choose(mates, turned)
     first, second, mates, mate_state = tie((first, second, mates, mate_state))
     guests = visit(parcel)
     beside = (first, swap(first), second, swap(second))
-    mate_part, *beside = attend(2, table, mates, beside, state=mate_state, pack=True, spare=2)
+    mate_part, *beside, _, _ = attend(2, table, mates, beside, state=mate_state, pack=True, spare=2)
     one = across(mate_part)
+    state = attend(3, table, turned, gathered=beside, state=(sums, stats))
     (guest_part,) = attend(4, table, guests, gathered=beside, pack=True)
     homeward = []
     for i in range(2, spots - 2):
         high, side = i // 2, i % 2
         homeward.append((i, (high - 1 + 2 * side) * 2 + 1 - side))
     two = lax.ppermute(guest_part, "blk", homeward)
-    state = attend(3, table, turned, gathered=beside, state=state)
     return merge(state, one, two)
 
 

time: 41.5 us -> 40.9 us (0.986)
  waiting for transfers between devices: 7.4 us -> 10.2 us
  starting transfers between devices: 15.6 us -> 13.6 us
  Pallas kernels: 18 us -> 17 us
    ppermute x1, waiting for transfers between devices: 0.01 us -> 1.36 us  [visit(): return lax.ppermute(value, ('blk', 'node'), pairs)]
    ppermute x2, starting transfers between devices: 2.77 us -> 1.42 us  [hop(): return lax.ppermute(value, 'blk', pairs)]
    pallas_call x5 -> x6, Pallas kernels: 15.3 us -> 14.3 us  [the longest x5 14.2 us: attend(): pl.pallas_call(functools.partial(attend_kernel, job * own, len(sources),...]
    ppermute x2, waiting for transfers between devices: 1.18 us -> 1.97 us  [hop(): return lax.ppermute(value, 'blk', pairs)]
    ppermute x1, waiting for transfers between devices: 5.26 us -> 6.01 us  [shards(): two = lax.ppermute(guest_part, 'blk', homeward)]
    ppermute x1, starting transfers between devices: 3.89 us -> 3.23 us  [shards(): two = lax.ppermute(guest_part, 'blk', homeward)]
  transfers between devices with their start and end apart: 9 -> 9, of which waited for: 5 -> 5; matrix products, arithmetic and copies ran while one was open for 0% -> 0% of each run, Pallas kernels for 38% -> 36%
where the time goes in v2:
time: 40.9 us
  Pallas kernels  17 us (42%)
  starting transfers between devices  13.6 us (33%)
  waiting for transfers between devices  10.2 us (25%)
    pallas_call x5, Pallas kernels, attend(): pl.pallas_call(functools.partial(attend_kernel, job * own, len(sources),...  14.2 us
    ppermute x2, starting transfers between devices, trade(): return lax.ppermute(value, ('blk', 'node'), pairs)  6.97 us
    ppermute x1, waiting for transfers between devices, shards(): two = lax.ppermute(guest_part, 'blk', homeward)  6.01 us
    ppermute x1, starting transfers between devices, shards(): two = lax.ppermute(guest_part, 'blk', homeward)  3.23 us
    ppermute x2, waiting for transfers between devices, hop(): return lax.ppermute(value, 'blk', pairs)  1.97 us
    ppermute x2, starting transfers between devices, hop(): return lax.ppermute(value, 'blk', pairs)  1.42 us
    ppermute x1, waiting for transfers between devices, visit(): return lax.ppermute(value, ('blk', 'node'), pairs)  1.36 us
    ppermute x1, starting transfers between devices, visit(): return lax.ppermute(value, ('blk', 'node'), pairs)  1.29 us
  transfers between devices with their start and end apart: 9, of which 5 were waited for; matrix products, arithmetic and copies ran while one was open for 0% of the time, Pallas kernels for 36%

profile of v2, /device:TPU:12, one launch (start us, length us, event | category | flops | bytes accessed | tf_op | source)
XLA Modules:
  0.0 40.9 jit_solution(467962249088221307)
XLA Ops:
  0.0 1.3 %bundle.1 = (bf16[2,1024,128]{2,1,0:T(8,128)(2,1)S(1)}, bf16[1024,128]{1,0:T(8,128)(2,1)S(1)}) custom-call(bf16[1024,128]{1,0:T(8,128)(2,1)} %q_ref.1, bf16[1024,128]{1,0:T(8,128)(2,1)} %k_ref.1, bf16[1024,128]{1,0:T(8,128)(2,1)} %v_ref.1), custom_call_target="tpu_custom_call" | custom-call | bytes 1048576 | tf_op jit(solution)/shard_map/bundle/pallas_call | solution.py:56
  1.3 0.1 collective-permute-start.3
  1.4 2.4 %collective-permute-start = (bf16[2,1024,128]{2,1,0:T(8,128)(2,1)S(1)}, bf16[2,1024,128]{2,1,0:T(8,128)(2,1)S(1)}, u32[]{:S(2)}, u32[]{:S(2)}) collective-permute-start(bf16[2,1024,128]{2,1,0:T(8,128)(2,1)S(1)} %get-tuple-element.24.refs_0_), channel_id=1, source_target_pairs={{0,4},{2,6},{4,0},{5,9},{6,2},{7,11},{8,12},{9,5},{10,14},{11,7},{... | collective-permute-start | bytes 1572872 | tf_op jit(solution)/shard_map/ppermute | solution.py:386
  3.7 4.6 %collective-permute-start.1 = (bf16[2,1024,128]{2,1,0:T(8,128)(2,1)S(1)}, bf16[2,1024,128]{2,1,0:T(8,128)(2,1)S(1)}, u32[]{:S(2)}, u32[]{:S(2)}) collective-permute-start(bf16[2,1024,128]{2,1,0:T(8,128)(2,1)S(1)} %get-tuple-element.24.refs_0_), channel_id=1, source_target_pairs={{1,5},{3,7},{4,8},{5,1},{6,10},{7,3},{8,4},{9,13},{10,6},{11,15},{... | collective-permute-start | bytes 1572872 | tf_op jit(solution)/shard_map/ppermute | solution.py:386
  8.4 0.6 %collective-permute-start.2 = (bf16[1024,128]{1,0:T(8,128)(2,1)S(1)}, bf16[1024,128]{1,0:T(8,128)(2,1)S(1)}, u32[]{:S(2)}, u32[]{:S(2)}) collective-permute-start(bf16[1024,128]{1,0:T(8,128)(2,1)S(1)} %get-tuple-element.23.q_ref.two_ref), channel_id=1, source_target_pairs={{0,2},{2,0},{4,6},{6,4},{8,10},{10,8},{12,14},{14,12},{1,3},{3,1},... | collective-permute-start | bytes 786440 | tf_op jit(solution)/shard_map/ppermute | solution.py:370
  8.9 0.5 %lists.1.list_ref = s32[40,128]{1,0:T(8,128)S(1)} custom-call(s32[128,128]{1,0:T(8,128)S(1)} %copy-done), custom_call_target="tpu_custom_call" | custom-call | flops 1000 | bytes 100000 | tf_op jit(solution)/shard_map/lists/pallas_call | solution.py:144
  9.5 0.0 collective-permute-done.3.refs_1_
  9.5 3.8 %attend0.1 = (bf16[2048,128]{1,0:T(8,128)(2,1)S(1)}, bf16[2048,128]{1,0:T(8,128)(2,1)S(1)}, f32[1024,128]{1,0:T(8,128)S(1)}, f32[16,128]{1,0:T(8,128)S(1)}) custom-call(s32[40,128]{1,0:T(8,128)S(1)} %lists.1.list_ref, bf16[1024,128]{1,0:T(8,128)(2,1)S(1)} %get-tuple-element.23.q_ref.two_ref, bf16[2,1024,128]{2,1,0:T(8,128)(2,1)S(1)} %get-tuple-element.24.refs_0_, ...), custom_call_target="tpu_custom_call" | custom-call | flops 1048576 | bytes 65536 | tf_op jit(solution)/shard_map/attend0/pallas_call | solution.py:285
  13.3 2.0 %collective-permute-done.2.q_ref.one_ref = bf16[1024,128]{1,0:T(8,128)(2,1)S(1)} collective-permute-done((bf16[1024,128]{1,0:T(8,128)(2,1)S(1)}, bf16[1024,128]{1,0:T(8,128)(2,1)S(1)}, u32[]{:S(2)}, u32[]{:S(2)}) %collective-permute-start.2) | collective-permute-done | bytes 262176 | tf_op jit(solution)/shard_map/ppermute | solution.py:370
  15.3 2.8 %attend1.1 = (f32[1024,128]{1,0:T(8,128)S(1)}, f32[16,128]{1,0:T(8,128)S(1)}) custom-call(s32[40,128]{1,0:T(8,128)S(1)} %lists.1.list_ref, bf16[1024,128]{1,0:T(8,128)(2,1)S(1)} %collective-permute-done.2.q_ref.one_ref, bf16[2048,128]{1,0:T(8,128)(2,1)S(1)} %get-tuple-element.25.refs_0_, bf16[2048,128]{1,0:T(8,128)(2,1)S(1)} %get-tuple-element.26.refs_1_), custom_call_target="tpu_custom_call" | custom-call | flops 1048576 | bytes 65536 | tf_op jit(solution)/shard_map/attend1/pallas_call | solution.py:285
  18.1 0.0 collective-permute-done.1.refs_2_
  18.1 0.1 collective-permute-start.4
  18.2 0.5 %collective-permute-start.5 = (bf16[2,1024,128]{2,1,0:T(8,128)(2,1)S(1)}, bf16[2,1024,128]{2,1,0:T(8,128)(2,1)S(1)}, u32[]{:S(2)}, u32[]{:S(2)}) collective-permute-start(bf16[2,1024,128]{2,1,0:T(8,128)(2,1)S(1)} %collective-permute-done.1.refs_2_), channel_id=1, source_target_pairs={{0,1},{1,0},{2,3},{3,2},{4,5},{5,4},{6,7},{7,6},{8,9},{9,8},{10,11... | collective-permute-start | bytes 1572872 | tf_op jit(solution)/shard_map/ppermute | solution.py:376
  18.7 1.3 %collective-permute-start.7 = (bf16[1024,128]{1,0:T(8,128)(2,1)S(1)}, bf16[1024,128]{1,0:T(8,128)(2,1)S(1)}, u32[]{:S(2)}, u32[]{:S(2)}) collective-permute-start(bf16[1024,128]{1,0:T(8,128)(2,1)S(1)} %choose.1), channel_id=1, source_target_pairs={{0,4},{3,5},{4,8},{7,9},{9,7},{10,6},{13,11},{14,10},{16,20},{19,2... | collective-permute-start | bytes 786440 | tf_op jit(solution)/shard_map/ppermute | solution.py:397
  20.0 0.1 collective-permute-done.4.refs_1_
  20.1 0.7 %collective-permute-done.5.refs_3_ = bf16[2,1024,128]{2,1,0:T(8,128)(2,1)S(1)} collective-permute-done((bf16[2,1024,128]{2,1,0:T(8,128)(2,1)S(1)}, bf16[2,1024,128]{2,1,0:T(8,128)(2,1)S(1)}, u32[]{:S(2)}, u32[]{:S(2)}) %collective-permute-start.5) | collective-permute-done | bytes 524320 | tf_op jit(solution)/shard_map/ppermute | solution.py:376
  20.8 3.9 %attend2.1 = (bf16[1104,128]{1,0:T(8,128)(2,1)S(1)}, bf16[4096,128]{1,0:T(8,128)(2,1)S(1)}, bf16[4096,128]{1,0:T(8,128)(2,1)S(1)}, f32[1024,128]{1,0:T(8,128)S(1)}, f32[16,128]{1,0:T(8,128)S(1)}) custom-call(s32[40,128]{1,0:T(8,128)S(1)} %lists.1.list_ref, ...), custom_call_target="tpu_custom_call", output_to_operand_aliasing={{3}: (6, {}), {4}: (7, {})} | custom-call | flops 1048576 | bytes 65536 | tf_op jit(solution)/shard_map/attend2/pallas_call | solution.py:285
  24.7 0.9 %collective-permute-start.6 = (bf16[1104,128]{1,0:T(8,128)(2,1)S(1)}, bf16[1104,128]{1,0:T(8,128)(2,1)S(1)}, u32[]{:S(2)}, u32[]{:S(2)}) collective-permute-start(bf16[1104,128]{1,0:T(8,128)(2,1)S(1)} %get-tuple-element.40), channel_id=1, source_target_pairs={{0,2},{2,0},{4,6},{6,4},{8,10},{10,8},{12,14},{14,12},{1,3},{3,1},... | collective-permute-start | bytes 847880 | tf_op jit(solution)/shard_map/ppermute | solution.py:370
  25.6 1.4 %collective-permute-done.7.q_ref = bf16[1024,128]{1,0:T(8,128)(2,1)S(1)} collective-permute-done((bf16[1024,128]{1,0:T(8,128)(2,1)S(1)}, bf16[1024,128]{1,0:T(8,128)(2,1)S(1)}, u32[]{:S(2)}, u32[]{:S(2)}) %collective-permute-start.7) | collective-permute-done | bytes 262176 | tf_op jit(solution)/shard_map/ppermute | solution.py:397
  27.0 1.9 %attend4.1 = bf16[1072,128]{1,0:T(8,128)(2,1)S(1)} custom-call(s32[40,128]{1,0:T(8,128)S(1)} %lists.1.list_ref, bf16[1024,128]{1,0:T(8,128)(2,1)S(1)} %collective-permute-done.7.q_ref, bf16[4096,128]{1,0:T(8,128)(2,1)S(1)} %get-tuple-element.34.refs_0_, bf16[4096,128]{1,0:T(8,128)(2,1)S(1)} %get-tuple-element.35.refs_1_), custom_call_target="tpu_custom_call" | custom-call | flops 1048576 | bytes 65536 | tf_op jit(solution)/shard_map/attend4/pallas_call | solution.py:285
  28.9 3.2 %collective-permute-start.8 = (bf16[1072,128]{1,0:T(8,128)(2,1)S(1)}, bf16[1072,128]{1,0:T(8,128)(2,1)S(1)}, u32[]{:S(2)}, u32[]{:S(2)}) collective-permute-start(bf16[1072,128]{1,0:T(8,128)(2,1)S(1)} %attend4.1), channel_id=1, source_target_pairs={{4,2},{6,8},{8,6},{10,12},{5,3},{7,9},{9,7},{11,13},{20,18},{22,24... | collective-permute-start | bytes 823304 | tf_op jit(solution)/shard_map/ppermute | solution.py:420
  32.1 1.8 %attend3.1 = (f32[1024,128]{1,0:T(8,128)S(1)}, f32[16,128]{1,0:T(8,128)S(1)}) custom-call(s32[40,128]{1,0:T(8,128)S(1)} %lists.1.list_ref, bf16[1024,128]{1,0:T(8,128)(2,1)S(1)} %get-tuple-element.23.q_ref.two_ref, bf16[4096,128]{1,0:T(8,128)(2,1)S(1)} %get-tuple-element.34.refs_0_, ...), custom_call_target="tpu_custom_call", output_to_operand_aliasing={{0}: (4, {}), {1}: (5, {})} | custom-call | flops 1048576 | bytes 65536 | tf_op jit(solution)/shard_map/attend3/pallas_call | solution.py:285
  33.9 6.0 %collective-permute-done.8.refs_1_ = bf16[1072,128]{1,0:T(8,128)(2,1)S(1)} collective-permute-done((bf16[1072,128]{1,0:T(8,128)(2,1)S(1)}, bf16[1072,128]{1,0:T(8,128)(2,1)S(1)}, u32[]{:S(2)}, u32[]{:S(2)}) %collective-permute-start.8) | collective-permute-done | bytes 274464 | tf_op jit(solution)/shard_map/ppermute | solution.py:420
  40.0 0.9 %merge.1 = bf16[1024,128]{1,0:T(8,128)(2,1)} custom-call(f32[1024,128]{1,0:T(8,128)S(1)} %get-tuple-element.38.sum_ref, f32[16,128]{1,0:T(8,128)S(1)} %get-tuple-element.39.stat_ref, bf16[1104,128]{1,0:T(8,128)(2,1)S(1)} %collective-permute-done.6.refs_0_, bf16[1072,128]{1,0:T(8,128)(2,1)S(1)} %collective-permute-done.8.refs_1_), custom_call_target="tpu_custom_call" | custom-call | flops 1048576 | bytes 1310720 | tf_op jit(solution)/shard_map/merge/pallas_call | solution.py:347
  (5 shorter events, 0.0 us)
Async XLA Ops:
  0.0 8.9 %copy-start = (s32[128,128]{1,0:T(8,128)S(1)}, s32[128,128]{1,0:T(8,128)}, u32[]{:S(2)}) copy-start(s32[128,128]{1,0:T(8,128)} %allowed_ref.1) | copy-start | bytes 196612
  1.3 8.2 %collective-permute-start.3 = (bf16[2,1024,128]{2,1,0:T(8,128)(2,1)S(1)}, bf16[2,1024,128]{2,1,0:T(8,128)(2,1)S(1)}, u32[]{:S(2)}, u32[]{:S(2)}) collective-permute-start(bf16[2,1024,128]{2,1,0:T(8,128)(2,1)S(1)} %get-tuple-element.24.refs_0_), channel_id=1, source_target_pairs={{0,1},{1,0},{2,3},{3,2},{4,5},{5,4},{6,7},{7,6},{8,9},{9,8},{10,11... | collective-permute-start | bytes 1572872 | tf_op jit(solution)/shard_map/ppermute | solution.py:376
  1.4 16.7 %collective-permute-start = (bf16[2,1024,128]{2,1,0:T(8,128)(2,1)S(1)}, bf16[2,1024,128]{2,1,0:T(8,128)(2,1)S(1)}, u32[]{:S(2)}, u32[]{:S(2)}) collective-permute-start(bf16[2,1024,128]{2,1,0:T(8,128)(2,1)S(1)} %get-tuple-element.24.refs_0_), channel_id=1, source_target_pairs={{0,4},{2,6},{4,0},{5,9},{6,2},{7,11},{8,12},{9,5},{10,14},{11,7},{... | collective-permute-start | bytes 1572872 | tf_op jit(solution)/shard_map/ppermute | solution.py:386
  3.7 14.3 %collective-permute-start.1 = (bf16[2,1024,128]{2,1,0:T(8,128)(2,1)S(1)}, bf16[2,1024,128]{2,1,0:T(8,128)(2,1)S(1)}, u32[]{:S(2)}, u32[]{:S(2)}) collective-permute-start(bf16[2,1024,128]{2,1,0:T(8,128)(2,1)S(1)} %get-tuple-element.24.refs_0_), channel_id=1, source_target_pairs={{1,5},{3,7},{4,8},{5,1},{6,10},{7,3},{8,4},{9,13},{10,6},{11,15},{... | collective-permute-start | bytes 1572872 | tf_op jit(solution)/shard_map/ppermute | solution.py:386
  8.4 6.9 %collective-permute-start.2 = (bf16[1024,128]{1,0:T(8,128)(2,1)S(1)}, bf16[1024,128]{1,0:T(8,128)(2,1)S(1)}, u32[]{:S(2)}, u32[]{:S(2)}) collective-permute-start(bf16[1024,128]{1,0:T(8,128)(2,1)S(1)} %get-tuple-element.23.q_ref.two_ref), channel_id=1, source_target_pairs={{0,2},{2,0},{4,6},{6,4},{8,10},{10,8},{12,14},{14,12},{1,3},{3,1},... | collective-permute-start | bytes 786440 | tf_op jit(solution)/shard_map/ppermute | solution.py:370
  18.1 2.0 %collective-permute-start.4 = (bf16[2,1024,128]{2,1,0:T(8,128)(2,1)S(1)}, bf16[2,1024,128]{2,1,0:T(8,128)(2,1)S(1)}, u32[]{:S(2)}, u32[]{:S(2)}) collective-permute-start(bf16[2,1024,128]{2,1,0:T(8,128)(2,1)S(1)} %collective-permute-done.refs_0_), channel_id=1, source_target_pairs={{0,1},{1,0},{2,3},{3,2},{4,5},{5,4},{6,7},{7,6},{8,9},{9,8},{10,11... | collective-permute-start | bytes 1572872 | tf_op jit(solution)/shard_map/ppermute | solution.py:376
  18.2 2.6 %collective-permute-start.5 = (bf16[2,1024,128]{2,1,0:T(8,128)(2,1)S(1)}, bf16[2,1024,128]{2,1,0:T(8,128)(2,1)S(1)}, u32[]{:S(2)}, u32[]{:S(2)}) collective-permute-start(bf16[2,1024,128]{2,1,0:T(8,128)(2,1)S(1)} %collective-permute-done.1.refs_2_), channel_id=1, source_target_pairs={{0,1},{1,0},{2,3},{3,2},{4,5},{5,4},{6,7},{7,6},{8,9},{9,8},{10,11... | collective-permute-start | bytes 1572872 | tf_op jit(solution)/shard_map/ppermute | solution.py:376
  18.7 8.3 %collective-permute-start.7 = (bf16[1024,128]{1,0:T(8,128)(2,1)S(1)}, bf16[1024,128]{1,0:T(8,128)(2,1)S(1)}, u32[]{:S(2)}, u32[]{:S(2)}) collective-permute-start(bf16[1024,128]{1,0:T(8,128)(2,1)S(1)} %choose.1), channel_id=1, source_target_pairs={{0,4},{3,5},{4,8},{7,9},{9,7},{10,6},{13,11},{14,10},{16,20},{19,2... | collective-permute-start | bytes 786440 | tf_op jit(solution)/shard_map/ppermute | solution.py:397
  24.7 15.2 %collective-permute-start.6 = (bf16[1104,128]{1,0:T(8,128)(2,1)S(1)}, bf16[1104,128]{1,0:T(8,128)(2,1)S(1)}, u32[]{:S(2)}, u32[]{:S(2)}) collective-permute-start(bf16[1104,128]{1,0:T(8,128)(2,1)S(1)} %get-tuple-element.40), channel_id=1, source_target_pairs={{0,2},{2,0},{4,6},{6,4},{8,10},{10,8},{12,14},{14,12},{1,3},{3,1},... | collective-permute-start | bytes 847880 | tf_op jit(solution)/shard_map/ppermute | solution.py:370
  28.9 11.1 %collective-permute-start.8 = (bf16[1072,128]{1,0:T(8,128)(2,1)S(1)}, bf16[1072,128]{1,0:T(8,128)(2,1)S(1)}, u32[]{:S(2)}, u32[]{:S(2)}) collective-permute-start(bf16[1072,128]{1,0:T(8,128)(2,1)S(1)} %attend4.1), channel_id=1, source_target_pairs={{4,2},{6,8},{8,6},{10,12},{5,3},{7,9},{9,7},{11,13},{20,18},{22,24... | collective-permute-start | bytes 823304 | tf_op jit(solution)/shard_map/ppermute | solution.py:420

commit v3 on v2

--- a/solution.py
+++ b/solution.py
@@ -19,7 +19,6 @@
 ANY = pl.BlockSpec(memory_space=pl.ANY)
 HBM = pl.BlockSpec(memory_space=pltpu.HBM)
 VMEM = pl.BlockSpec(memory_space=pltpu.VMEM)
-SMEM = pl.BlockSpec(memory_space=pltpu.SMEM)
 
 
 def cost(flops, moved, exps=0):
@@ -172,7 +171,7 @@
     return jnp.where(total > 0, top, FLOOR), total
 
 
-def attend_kernel(base, sources, resume, pack, list_ref, q_ref, *refs):
+def attend_kernel(base, sources, resume, pack, table_ref, q_ref, *refs):
     rows = q_ref.shape[0]
     own = rows // BLOCK
     refs = list(refs)
@@ -186,7 +185,10 @@
         (out_ref,) = take(1)
     if sources:
         k_ref, v_ref = take(2)
-    sum_ref, stat_ref, sems = refs
+    sum_ref, stat_ref, list_ref, sems = refs
+    mine = table_ref.at[pl.ds(base, own), :]
+    load_list = pltpu.make_async_copy(mine, list_ref, sems.at[2 * sources])
+    load_list.start()
     copies = []
     for n, ref in enumerate(source_refs):
         at = pl.ds(n * rows, rows)
@@ -194,15 +196,16 @@
         copies.append(pltpu.make_async_copy(ref.at[1], v_ref.at[at, :], sems.at[2 * n + 1]))
     for copy in copies:
         copy.start()
-    counts = [list_ref[base + i, COUNT_AT] for i in range(own)]
+    if not resume:
+        sum_ref[...] = jnp.zeros_like(sum_ref)
+        stat_ref[pl.ds(0, own), :] = jnp.full((own, BLOCK), FLOOR, jnp.float32)
+        stat_ref[pl.ds(own, own), :] = jnp.zeros((own, BLOCK), jnp.float32)
+    load_list.wait()
+    counts = [list_ref[i, COUNT_AT] for i in range(own)]
     steps = counts[0]
     for count in counts[1:]:
         steps = jnp.maximum(steps, count)
     steps = (steps + WIDE - 1) // WIDE
-    if not resume:
-        sum_ref[...] = jnp.zeros_like(sum_ref)
-        stat_ref[pl.ds(0, own), :] = jnp.full((own, BLOCK), FLOOR, jnp.float32)
-        stat_ref[pl.ds(own, own), :] = jnp.zeros((own, BLOCK), jnp.float32)
     for copy in copies:
         copy.wait()
     tops = tuple(stat_ref[pl.ds(i, 1), :] for i in range(own))
@@ -219,7 +222,7 @@
             for u in range(WIDE):
                 at = t * WIDE + u
                 live = at < counts[i]
-                index = jnp.where(live, list_ref[base + i, at], 0)
+                index = jnp.where(live, list_ref[i, at], 0)
                 bias = jnp.where(live, jnp.float32(0.0), jnp.float32(DROP))
                 spot = pl.ds(pl.multiple_of(index * BLOCK, BLOCK), BLOCK)
                 score = jnp.dot(k_ref[spot, :], turned, preferred_element_type=jnp.float32)
@@ -285,9 +288,13 @@
     return pl.pallas_call(
         functools.partial(attend_kernel, job * own, len(sources), len(state) > 0, pack),
         out_shape=out_shape,
-        in_specs=[SMEM, VMEM] + [ANY] * len(sources) + [VMEM] * len(direct),
+        in_specs=[ANY, VMEM] + [ANY] * len(sources) + [VMEM] * len(direct),
         out_specs=[VMEM] * outs,
-        scratch_shapes=scratch + [pltpu.SemaphoreType.DMA((max(1, 2 * len(sources)),))],
+        scratch_shapes=scratch
+        + [
+            pltpu.SMEM((own, table.shape[1]), jnp.int32),
+            pltpu.SemaphoreType.DMA((2 * len(sources) + 1,)),
+        ],
         input_output_aliases=aliases,
         cost_estimate=cost(1 << 20, 1 << 16),
         compiler_params=grant(8),

time: 40.9 us -> 40.4 us (0.988)
  Pallas kernels: 17 us -> 14.5 us
  starting transfers between devices: 13.6 us -> 14.8 us
  waiting for transfers between devices: 10.2 us -> 10.8 us
    pallas_call x5, Pallas kernels: 14.2 us -> 11.7 us  [attend(): pl.pallas_call(functools.partial(attend_kernel, job * own, len(sources),...]
    ppermute x2, starting transfers between devices: 1.42 us -> 2.54 us  [hop(): return lax.ppermute(value, 'blk', pairs)]
    ppermute x2, waiting for transfers between devices: 0.01 us -> 0.72 us  [trade(): return lax.ppermute(value, ('blk', 'node'), pairs)]
    ppermute x1, waiting for transfers between devices: 6.01 us -> 5.41 us  [shards(): two = lax.ppermute(guest_part, 'blk', homeward)]
  transfers between devices with their start and end apart: 9 -> 9, of which waited for: 5 -> 6; matrix products, arithmetic and copies ran while one was open for 0% -> 0% of each run, Pallas kernels for 36% -> 31%
where the time goes in v3:
time: 40.4 us; the launch traced here: 40.2 us
  starting transfers between devices  14.8 us (37%)
  Pallas kernels  14.5 us (36%)
  waiting for transfers between devices  10.8 us (27%)
    pallas_call x5, Pallas kernels, attend(): pl.pallas_call(functools.partial(attend_kernel, job * own, len(sources),...  11.7 us
    ppermute x2, starting transfers between devices, trade(): return lax.ppermute(value, ('blk', 'node'), pairs)  6.97 us
    ppermute x1, waiting for transfers between devices, shards(): two = lax.ppermute(guest_part, 'blk', homeward)  5.41 us
    ppermute x1, starting transfers between devices, shards(): two = lax.ppermute(guest_part, 'blk', homeward)  3.43 us
    ppermute x2, starting transfers between devices, hop(): return lax.ppermute(value, 'blk', pairs)  2.54 us
    ppermute x2, waiting for transfers between devices, hop(): return lax.ppermute(value, 'blk', pairs)  2.31 us
    ppermute x1, waiting for transfers between devices, visit(): return lax.ppermute(value, ('blk', 'node'), pairs)  1.57 us
    ppermute x1, starting transfers between devices, visit(): return lax.ppermute(value, ('blk', 'node'), pairs)  1.29 us
  transfers between devices with their start and end apart: 9, of which 6 were waited for; matrix products, arithmetic and copies ran while one was open for 0% of the time, Pallas kernels for 31%

profile of v3, /device:TPU:12, one launch (start us, length us, event | category | flops | bytes accessed | tf_op | source)
XLA Modules:
  0.0 40.2 jit_solution(8843190241614514004)
XLA Ops:
  0.0 1.3 %bundle.1 = (bf16[2,1024,128]{2,1,0:T(8,128)(2,1)S(1)}, bf16[1024,128]{1,0:T(8,128)(2,1)S(1)}) custom-call(bf16[1024,128]{1,0:T(8,128)(2,1)} %q_ref.1, bf16[1024,128]{1,0:T(8,128)(2,1)} %k_ref.1, bf16[1024,128]{1,0:T(8,128)(2,1)} %v_ref.1), custom_call_target="tpu_custom_call" | custom-call | bytes 1048576 | tf_op jit(solution)/shard_map/bundle/pallas_call | solution.py:55
  1.3 0.1 collective-permute-start.3
  1.4 2.4 %collective-permute-start = (bf16[2,1024,128]{2,1,0:T(8,128)(2,1)S(1)}, bf16[2,1024,128]{2,1,0:T(8,128)(2,1)S(1)}, u32[]{:S(2)}, u32[]{:S(2)}) collective-permute-start(bf16[2,1024,128]{2,1,0:T(8,128)(2,1)S(1)} %get-tuple-element.24.refs_0_), channel_id=1, source_target_pairs={{0,4},{2,6},{4,0},{5,9},{6,2},{7,11},{8,12},{9,5},{10,14},{11,7},{... | collective-permute-start | bytes 1572872 | tf_op jit(solution)/shard_map/ppermute | solution.py:393
  3.7 4.6 %collective-permute-start.1 = (bf16[2,1024,128]{2,1,0:T(8,128)(2,1)S(1)}, bf16[2,1024,128]{2,1,0:T(8,128)(2,1)S(1)}, u32[]{:S(2)}, u32[]{:S(2)}) collective-permute-start(bf16[2,1024,128]{2,1,0:T(8,128)(2,1)S(1)} %get-tuple-element.24.refs_0_), channel_id=1, source_target_pairs={{1,5},{3,7},{4,8},{5,1},{6,10},{7,3},{8,4},{9,13},{10,6},{11,15},{... | collective-permute-start | bytes 1572872 | tf_op jit(solution)/shard_map/ppermute | solution.py:393
  8.4 0.6 %collective-permute-start.2 = (bf16[1024,128]{1,0:T(8,128)(2,1)S(1)}, bf16[1024,128]{1,0:T(8,128)(2,1)S(1)}, u32[]{:S(2)}, u32[]{:S(2)}) collective-permute-start(bf16[1024,128]{1,0:T(8,128)(2,1)S(1)} %get-tuple-element.23.q_ref.two_ref), channel_id=1, source_target_pairs={{0,2},{2,0},{4,6},{6,4},{8,10},{10,8},{12,14},{14,12},{1,3},{3,1},... | collective-permute-start | bytes 786440 | tf_op jit(solution)/shard_map/ppermute | solution.py:377
  8.9 0.5 %lists.1.table_ref = s32[40,128]{1,0:T(8,128)S(1)} custom-call(s32[128,128]{1,0:T(8,128)S(1)} %copy-done), custom_call_target="tpu_custom_call" | custom-call | flops 1000 | bytes 100000 | tf_op jit(solution)/shard_map/lists/pallas_call | solution.py:143
  9.5 0.0 collective-permute-done.3.refs_1_
  9.5 3.5 %attend0.1 = (bf16[2048,128]{1,0:T(8,128)(2,1)S(1)}, bf16[2048,128]{1,0:T(8,128)(2,1)S(1)}, f32[1024,128]{1,0:T(8,128)S(1)}, f32[16,128]{1,0:T(8,128)S(1)}) custom-call(s32[40,128]{1,0:T(8,128)S(1)} %lists.1.table_ref, bf16[1024,128]{1,0:T(8,128)(2,1)S(1)} %get-tuple-element.23.q_ref.two_ref, bf16[2,1024,128]{2,1,0:T(8,128)(2,1)S(1)} %get-tuple-element.24.refs_0_, ...), custom_call_target="tpu_custom_call" | custom-call | flops 1048576 | bytes 65536 | tf_op jit(solution)/shard_map/attend0/pallas_call | solution.py:288
  13.0 2.3 %collective-permute-done.2.q_ref.one_ref = bf16[1024,128]{1,0:T(8,128)(2,1)S(1)} collective-permute-done((bf16[1024,128]{1,0:T(8,128)(2,1)S(1)}, bf16[1024,128]{1,0:T(8,128)(2,1)S(1)}, u32[]{:S(2)}, u32[]{:S(2)}) %collective-permute-start.2) | collective-permute-done | bytes 262176 | tf_op jit(solution)/shard_map/ppermute | solution.py:377
  15.3 1.6 %attend1.1 = (f32[1024,128]{1,0:T(8,128)S(1)}, f32[16,128]{1,0:T(8,128)S(1)}) custom-call(s32[40,128]{1,0:T(8,128)S(1)} %lists.1.table_ref, bf16[1024,128]{1,0:T(8,128)(2,1)S(1)} %collective-permute-done.2.q_ref.one_ref, bf16[2048,128]{1,0:T(8,128)(2,1)S(1)} %get-tuple-element.25.refs_0_, bf16[2048,128]{1,0:T(8,128)(2,1)S(1)} %get-tuple-element.26.refs_1_), custom_call_target="tpu_custom_call" | custom-call | flops 1048576 | bytes 65536 | tf_op jit(solution)/shard_map/attend1/pallas_call | solution.py:288
  16.9 0.7 %collective-permute-done.1.refs_2_ = bf16[2,1024,128]{2,1,0:T(8,128)(2,1)S(1)} collective-permute-done((bf16[2,1024,128]{2,1,0:T(8,128)(2,1)S(1)}, bf16[2,1024,128]{2,1,0:T(8,128)(2,1)S(1)}, u32[]{:S(2)}, u32[]{:S(2)}) %collective-permute-start.1) | collective-permute-done | bytes 524320 | tf_op jit(solution)/shard_map/ppermute | solution.py:393
  17.6 0.3 collective-permute-start.4
  17.9 0.2 collective-permute-start.5
  18.1 1.3 %collective-permute-start.7 = (bf16[1024,128]{1,0:T(8,128)(2,1)S(1)}, bf16[1024,128]{1,0:T(8,128)(2,1)S(1)}, u32[]{:S(2)}, u32[]{:S(2)}) collective-permute-start(bf16[1024,128]{1,0:T(8,128)(2,1)S(1)} %choose.1), channel_id=1, source_target_pairs={{0,4},{3,5},{4,8},{7,9},{9,7},{10,6},{13,11},{14,10},{16,20},{19,2... | collective-permute-start | bytes 786440 | tf_op jit(solution)/shard_map/ppermute | solution.py:404
  19.4 0.1 collective-permute-done.4.refs_1_
  19.5 0.7 %collective-permute-done.5.refs_3_ = bf16[2,1024,128]{2,1,0:T(8,128)(2,1)S(1)} collective-permute-done((bf16[2,1024,128]{2,1,0:T(8,128)(2,1)S(1)}, bf16[2,1024,128]{2,1,0:T(8,128)(2,1)S(1)}, u32[]{:S(2)}, u32[]{:S(2)}) %collective-permute-start.5) | collective-permute-done | bytes 524320 | tf_op jit(solution)/shard_map/ppermute | solution.py:383
  20.2 2.6 %attend2.1 = (bf16[1104,128]{1,0:T(8,128)(2,1)S(1)}, bf16[4096,128]{1,0:T(8,128)(2,1)S(1)}, bf16[4096,128]{1,0:T(8,128)(2,1)S(1)}, f32[1024,128]{1,0:T(8,128)S(1)}, f32[16,128]{1,0:T(8,128)S(1)}) custom-call(s32[40,128]{1,0:T(8,128)S(1)} %lists.1.table_ref, ...), custom_call_target="tpu_custom_call", output_to_operand_aliasing={{3}: (6, {}), {4}: (7, {})} | custom-call | flops 1048576 | bytes 65536 | tf_op jit(solution)/shard_map/attend2/pallas_call | solution.py:288
  22.9 2.0 %collective-permute-start.6 = (bf16[1104,128]{1,0:T(8,128)(2,1)S(1)}, bf16[1104,128]{1,0:T(8,128)(2,1)S(1)}, u32[]{:S(2)}, u32[]{:S(2)}) collective-permute-start(bf16[1104,128]{1,0:T(8,128)(2,1)S(1)} %get-tuple-element.40), channel_id=1, source_target_pairs={{0,2},{2,0},{4,6},{6,4},{8,10},{10,8},{12,14},{14,12},{1,3},{3,1},... | collective-permute-start | bytes 847880 | tf_op jit(solution)/shard_map/ppermute | solution.py:377
  24.8 1.6 %collective-permute-done.7.q_ref = bf16[1024,128]{1,0:T(8,128)(2,1)S(1)} collective-permute-done((bf16[1024,128]{1,0:T(8,128)(2,1)S(1)}, bf16[1024,128]{1,0:T(8,128)(2,1)S(1)}, u32[]{:S(2)}, u32[]{:S(2)}) %collective-permute-start.7) | collective-permute-done | bytes 262176 | tf_op jit(solution)/shard_map/ppermute | solution.py:404
  26.4 1.6 %attend4.1 = bf16[1072,128]{1,0:T(8,128)(2,1)S(1)} custom-call(s32[40,128]{1,0:T(8,128)S(1)} %lists.1.table_ref, bf16[1024,128]{1,0:T(8,128)(2,1)S(1)} %collective-permute-done.7.q_ref, bf16[4096,128]{1,0:T(8,128)(2,1)S(1)} %get-tuple-element.34.refs_0_, bf16[4096,128]{1,0:T(8,128)(2,1)S(1)} %get-tuple-element.35.refs_1_), custom_call_target="tpu_custom_call" | custom-call | flops 1048576 | bytes 65536 | tf_op jit(solution)/shard_map/attend4/pallas_call | solution.py:288
  28.0 3.4 %collective-permute-start.8 = (bf16[1072,128]{1,0:T(8,128)(2,1)S(1)}, bf16[1072,128]{1,0:T(8,128)(2,1)S(1)}, u32[]{:S(2)}, u32[]{:S(2)}) collective-permute-start(bf16[1072,128]{1,0:T(8,128)(2,1)S(1)} %attend4.1), channel_id=1, source_target_pairs={{4,2},{6,8},{8,6},{10,12},{5,3},{7,9},{9,7},{11,13},{20,18},{22,24... | collective-permute-start | bytes 823304 | tf_op jit(solution)/shard_map/ppermute | solution.py:427
  31.4 2.5 %attend3.1 = (f32[1024,128]{1,0:T(8,128)S(1)}, f32[16,128]{1,0:T(8,128)S(1)}) custom-call(s32[40,128]{1,0:T(8,128)S(1)} %lists.1.table_ref, bf16[1024,128]{1,0:T(8,128)(2,1)S(1)} %get-tuple-element.23.q_ref.two_ref, bf16[4096,128]{1,0:T(8,128)(2,1)S(1)} %get-tuple-element.34.refs_0_, ...), custom_call_target="tpu_custom_call", output_to_operand_aliasing={{0}: (4, {}), {1}: (5, {})} | custom-call | flops 1048576 | bytes 65536 | tf_op jit(solution)/shard_map/attend3/pallas_call | solution.py:288
  33.9 5.4 %collective-permute-done.8.refs_1_ = bf16[1072,128]{1,0:T(8,128)(2,1)S(1)} collective-permute-done((bf16[1072,128]{1,0:T(8,128)(2,1)S(1)}, bf16[1072,128]{1,0:T(8,128)(2,1)S(1)}, u32[]{:S(2)}, u32[]{:S(2)}) %collective-permute-start.8) | collective-permute-done | bytes 274464 | tf_op jit(solution)/shard_map/ppermute | solution.py:427
  39.3 0.9 %merge.1 = bf16[1024,128]{1,0:T(8,128)(2,1)} custom-call(f32[1024,128]{1,0:T(8,128)S(1)} %get-tuple-element.38.sum_ref, f32[16,128]{1,0:T(8,128)S(1)} %get-tuple-element.39.stat_ref, bf16[1104,128]{1,0:T(8,128)(2,1)S(1)} %collective-permute-done.6.refs_0_, bf16[1072,128]{1,0:T(8,128)(2,1)S(1)} %collective-permute-done.8.refs_1_), custom_call_target="tpu_custom_call" | custom-call | flops 1048576 | bytes 1310720 | tf_op jit(solution)/shard_map/merge/pallas_call | solution.py:354
  (5 shorter events, 0.0 us)
Async XLA Ops:
  0.0 8.9 %copy-start = (s32[128,128]{1,0:T(8,128)S(1)}, s32[128,128]{1,0:T(8,128)}, u32[]{:S(2)}) copy-start(s32[128,128]{1,0:T(8,128)} %allowed_ref.1) | copy-start | bytes 196612
  1.3 8.2 %collective-permute-start.3 = (bf16[2,1024,128]{2,1,0:T(8,128)(2,1)S(1)}, bf16[2,1024,128]{2,1,0:T(8,128)(2,1)S(1)}, u32[]{:S(2)}, u32[]{:S(2)}) collective-permute-start(bf16[2,1024,128]{2,1,0:T(8,128)(2,1)S(1)} %get-tuple-element.24.refs_0_), channel_id=1, source_target_pairs={{0,1},{1,0},{2,3},{3,2},{4,5},{5,4},{6,7},{7,6},{8,9},{9,8},{10,11... | collective-permute-start | bytes 1572872 | tf_op jit(solution)/shard_map/ppermute | solution.py:383
  1.4 15.5 %collective-permute-start = (bf16[2,1024,128]{2,1,0:T(8,128)(2,1)S(1)}, bf16[2,1024,128]{2,1,0:T(8,128)(2,1)S(1)}, u32[]{:S(2)}, u32[]{:S(2)}) collective-permute-start(bf16[2,1024,128]{2,1,0:T(8,128)(2,1)S(1)} %get-tuple-element.24.refs_0_), channel_id=1, source_target_pairs={{0,4},{2,6},{4,0},{5,9},{6,2},{7,11},{8,12},{9,5},{10,14},{11,7},{... | collective-permute-start | bytes 1572872 | tf_op jit(solution)/shard_map/ppermute | solution.py:393
  3.7 13.8 %collective-permute-start.1 = (bf16[2,1024,128]{2,1,0:T(8,128)(2,1)S(1)}, bf16[2,1024,128]{2,1,0:T(8,128)(2,1)S(1)}, u32[]{:S(2)}, u32[]{:S(2)}) collective-permute-start(bf16[2,1024,128]{2,1,0:T(8,128)(2,1)S(1)} %get-tuple-element.24.refs_0_), channel_id=1, source_target_pairs={{1,5},{3,7},{4,8},{5,1},{6,10},{7,3},{8,4},{9,13},{10,6},{11,15},{... | collective-permute-start | bytes 1572872 | tf_op jit(solution)/shard_map/ppermute | solution.py:393
  8.4 6.9 %collective-permute-start.2 = (bf16[1024,128]{1,0:T(8,128)(2,1)S(1)}, bf16[1024,128]{1,0:T(8,128)(2,1)S(1)}, u32[]{:S(2)}, u32[]{:S(2)}) collective-permute-start(bf16[1024,128]{1,0:T(8,128)(2,1)S(1)} %get-tuple-element.23.q_ref.two_ref), channel_id=1, source_target_pairs={{0,2},{2,0},{4,6},{6,4},{8,10},{10,8},{12,14},{14,12},{1,3},{3,1},... | collective-permute-start | bytes 786440 | tf_op jit(solution)/shard_map/ppermute | solution.py:377
  17.6 1.9 %collective-permute-start.4 = (bf16[2,1024,128]{2,1,0:T(8,128)(2,1)S(1)}, bf16[2,1024,128]{2,1,0:T(8,128)(2,1)S(1)}, u32[]{:S(2)}, u32[]{:S(2)}) collective-permute-start(bf16[2,1024,128]{2,1,0:T(8,128)(2,1)S(1)} %collective-permute-done.refs_0_), channel_id=1, source_target_pairs={{0,1},{1,0},{2,3},{3,2},{4,5},{5,4},{6,7},{7,6},{8,9},{9,8},{10,11... | collective-permute-start | bytes 1572872 | tf_op jit(solution)/shard_map/ppermute | solution.py:383
  17.9 2.4 %collective-permute-start.5 = (bf16[2,1024,128]{2,1,0:T(8,128)(2,1)S(1)}, bf16[2,1024,128]{2,1,0:T(8,128)(2,1)S(1)}, u32[]{:S(2)}, u32[]{:S(2)}) collective-permute-start(bf16[2,1024,128]{2,1,0:T(8,128)(2,1)S(1)} %collective-permute-done.1.refs_2_), channel_id=1, source_target_pairs={{0,1},{1,0},{2,3},{3,2},{4,5},{5,4},{6,7},{7,6},{8,9},{9,8},{10,11... | collective-permute-start | bytes 1572872 | tf_op jit(solution)/shard_map/ppermute | solution.py:383
  18.1 8.3 %collective-permute-start.7 = (bf16[1024,128]{1,0:T(8,128)(2,1)S(1)}, bf16[1024,128]{1,0:T(8,128)(2,1)S(1)}, u32[]{:S(2)}, u32[]{:S(2)}) collective-permute-start(bf16[1024,128]{1,0:T(8,128)(2,1)S(1)} %choose.1), channel_id=1, source_target_pairs={{0,4},{3,5},{4,8},{7,9},{9,7},{10,6},{13,11},{14,10},{16,20},{19,2... | collective-permute-start | bytes 786440 | tf_op jit(solution)/shard_map/ppermute | solution.py:404
  22.9 16.5 %collective-permute-start.6 = (bf16[1104,128]{1,0:T(8,128)(2,1)S(1)}, bf16[1104,128]{1,0:T(8,128)(2,1)S(1)}, u32[]{:S(2)}, u32[]{:S(2)}) collective-permute-start(bf16[1104,128]{1,0:T(8,128)(2,1)S(1)} %get-tuple-element.40), channel_id=1, source_target_pairs={{0,2},{2,0},{4,6},{6,4},{8,10},{10,8},{12,14},{14,12},{1,3},{3,1},... | collective-permute-start | bytes 847880 | tf_op jit(solution)/shard_map/ppermute | solution.py:377
  28.0 11.3 %collective-permute-start.8 = (bf16[1072,128]{1,0:T(8,128)(2,1)S(1)}, bf16[1072,128]{1,0:T(8,128)(2,1)S(1)}, u32[]{:S(2)}, u32[]{:S(2)}) collective-permute-start(bf16[1072,128]{1,0:T(8,128)(2,1)S(1)} %attend4.1), channel_id=1, source_target_pairs={{4,2},{6,8},{8,6},{10,12},{5,3},{7,9},{9,7},{11,13},{20,18},{22,24... | collective-permute-start | bytes 823304 | tf_op jit(solution)/shard_map/ppermute | solution.py:427

commit v4 on v3

--- a/solution.py
+++ b/solution.py
@@ -14,7 +14,7 @@
 DROP = -3e38
 FACTOR = HEAD ** (-0.5) * math.log2(math.e)
 COUNT_AT = 64
-WIDE = 4
+WIDTHS = (4, 4, 5, 4, 4)
 
 ANY = pl.BlockSpec(memory_space=pl.ANY)
 HBM = pl.BlockSpec(memory_space=pltpu.HBM)
@@ -171,7 +171,7 @@
     return jnp.where(total > 0, top, FLOOR), total
 
 
-def attend_kernel(base, sources, resume, pack, table_ref, q_ref, *refs):
+def attend_kernel(base, wide, sources, resume, pack, table_ref, q_ref, *refs):
     rows = q_ref.shape[0]
     own = rows // BLOCK
     refs = list(refs)
@@ -205,7 +205,7 @@
     steps = counts[0]
     for count in counts[1:]:
         steps = jnp.maximum(steps, count)
-    steps = (steps + WIDE - 1) // WIDE
+    steps = (steps + wide - 1) // wide
     for copy in copies:
         copy.wait()
     tops = tuple(stat_ref[pl.ds(i, 1), :] for i in range(own))
@@ -219,8 +219,8 @@
             turned = q_ref[mine, :]
             spots, scores, biases = [], [], []
             top = tops[i]
-            for u in range(WIDE):
-                at = t * WIDE + u
+            for u in range(wide):
+                at = t * wide + u
                 live = at < counts[i]
                 index = jnp.where(live, list_ref[i, at], 0)
                 bias = jnp.where(live, jnp.float32(0.0), jnp.float32(DROP))
@@ -286,7 +286,7 @@
     outs = len(out_shape)
     aliases = {operands - 2: outs - 2, operands - 1: outs - 1} if state else {}
     return pl.pallas_call(
-        functools.partial(attend_kernel, job * own, len(sources), len(state) > 0, pack),
+        functools.partial(attend_kernel, job * own, WIDTHS[job], len(sources), len(state) > 0, pack),
         out_shape=out_shape,
         in_specs=[ANY, VMEM] + [ANY] * len(sources) + [VMEM] * len(direct),
         out_specs=[VMEM] * outs,
@@ -327,7 +327,7 @@
 
 
 def merge_kernel(sum_ref, stat_ref, *refs):
-    *other_refs, out_ref = refs
+    *other_refs, out_ref, done_ref, sems = refs
     rows = sum_ref.shape[0]
     own = rows // BLOCK
     top0, total0 = stat_ref[pl.ds(0, own), :], stat_ref[pl.ds(own, own), :]
@@ -340,13 +340,19 @@
     inverse = 1.0 / sum(shares, share * total0)
     share = share * inverse
     shares = [x * inverse for x in shares]
+    copies = []
     for i in range(own):
         mine = pl.ds(i * BLOCK, BLOCK)
         row = slice(i, i + 1)
         mixed = sum_ref[mine, :] * share[row]
         for ref, part in zip(other_refs, shares):
             mixed = mixed + ref[mine, :].astype(jnp.float32) * part[row]
-        out_ref[mine, :] = mixed.astype(jnp.bfloat16).T
+        done_ref[mine, :] = mixed.astype(jnp.bfloat16).T
+        copy = pltpu.make_async_copy(done_ref.at[mine, :], out_ref.at[mine, :], sems.at[i])
+        copy.start()
+        copies.append(copy)
+    for copy in copies:
+        copy.wait()
 
 
 def merge(state, *others):
@@ -355,7 +361,11 @@
         merge_kernel,
         out_shape=jax.ShapeDtypeStruct((rows, HEAD), jnp.bfloat16),
         in_specs=[VMEM] * (2 + len(others)),
-        out_specs=VMEM,
+        out_specs=ANY,
+        scratch_shapes=[
+            pltpu.VMEM((rows, HEAD), jnp.bfloat16),
+            pltpu.SemaphoreType.DMA((rows // BLOCK,)),
+        ],
         cost_estimate=cost(8 * rows * HEAD, 10 * rows * HEAD),
         compiler_params=grant(4),
         name="merge",

time: 40.4 us -> 40.5 us (level)
  waiting for transfers between devices: 10.8 us -> 12.5 us
  starting transfers between devices: 14.8 us -> 13.7 us
  Pallas kernels: 14.5 us -> 13.9 us
    ppermute x2, starting transfers between devices: 2.54 us -> 1.46 us  [hop(): return lax.ppermute(value, 'blk', pairs)]
    ppermute x1, waiting for transfers between devices: 5.41 us -> 6.36 us  [shards(): two = lax.ppermute(guest_part, 'blk', homeward)]
    ppermute x1, waiting for transfers between devices: 1.57 us -> 2.32 us  [visit(): return lax.ppermute(value, ('blk', 'node'), pairs)]
    pallas_call x5, Pallas kernels: 11.7 us -> 11.1 us  [attend(): pl.pallas_call(functools.partial(attend_kernel, job * own, WIDTHS[job], l...]
  transfers between devices with their start and end apart: 9 -> 9, of which waited for: 6 -> 6; matrix products, arithmetic and copies ran while one was open for 0% -> 0% of each run, Pallas kernels for 31% -> 29%
where the time goes in v4:
time: 40.5 us; the launch traced here: 40.3 us
  Pallas kernels  13.9 us (34%)
  starting transfers between devices  13.7 us (34%)
  waiting for transfers between devices  12.5 us (31%)
    pallas_call x5, Pallas kernels, attend(): pl.pallas_call(functools.partial(attend_kernel, job * own, WIDTHS[job], l...  11.1 us
    ppermute x2, starting transfers between devices, trade(): return lax.ppermute(value, ('blk', 'node'), pairs)  6.97 us
    ppermute x1, waiting for transfers between devices, shards(): two = lax.ppermute(guest_part, 'blk', homeward)  6.36 us
    ppermute x1, starting transfers between devices, shards(): two = lax.ppermute(guest_part, 'blk', homeward)  3.43 us
    ppermute x1, waiting for transfers between devices, visit(): return lax.ppermute(value, ('blk', 'node'), pairs)  2.32 us
    ppermute x2, waiting for transfers between devices, hop(): return lax.ppermute(value, 'blk', pairs)  2.31 us
    ppermute x2, starting transfers between devices, hop(): return lax.ppermute(value, 'blk', pairs)  1.46 us
    ppermute x1, starting transfers between devices, visit(): return lax.ppermute(value, ('blk', 'node'), pairs)  1.29 us
  transfers between devices with their start and end apart: 9, of which 6 were waited for; matrix products, arithmetic and copies ran while one was open for 0% of the time, Pallas kernels for 29%

profile of v4, /device:TPU:12, one launch (start us, length us, event | category | flops | bytes accessed | tf_op | source)
XLA Modules:
  0.0 40.3 jit_solution(16953273877719882800)
XLA Ops:
  0.0 1.3 %bundle.1 = (bf16[2,1024,128]{2,1,0:T(8,128)(2,1)S(1)}, bf16[1024,128]{1,0:T(8,128)(2,1)S(1)}) custom-call(bf16[1024,128]{1,0:T(8,128)(2,1)} %q_ref.1, bf16[1024,128]{1,0:T(8,128)(2,1)} %k_ref.1, bf16[1024,128]{1,0:T(8,128)(2,1)} %v_ref.1), custom_call_target="tpu_custom_call" | custom-call | bytes 1048576 | tf_op jit(solution)/shard_map/bundle/pallas_call | solution.py:55
  1.3 0.1 collective-permute-start.3
  1.4 2.4 %collective-permute-start = (bf16[2,1024,128]{2,1,0:T(8,128)(2,1)S(1)}, bf16[2,1024,128]{2,1,0:T(8,128)(2,1)S(1)}, u32[]{:S(2)}, u32[]{:S(2)}) collective-permute-start(bf16[2,1024,128]{2,1,0:T(8,128)(2,1)S(1)} %get-tuple-element.24.refs_0_), channel_id=1, source_target_pairs={{0,4},{2,6},{4,0},{5,9},{6,2},{7,11},{8,12},{9,5},{10,14},{11,7},{... | collective-permute-start | bytes 1572872 | tf_op jit(solution)/shard_map/ppermute | solution.py:403
  3.7 4.6 %collective-permute-start.1 = (bf16[2,1024,128]{2,1,0:T(8,128)(2,1)S(1)}, bf16[2,1024,128]{2,1,0:T(8,128)(2,1)S(1)}, u32[]{:S(2)}, u32[]{:S(2)}) collective-permute-start(bf16[2,1024,128]{2,1,0:T(8,128)(2,1)S(1)} %get-tuple-element.24.refs_0_), channel_id=1, source_target_pairs={{1,5},{3,7},{4,8},{5,1},{6,10},{7,3},{8,4},{9,13},{10,6},{11,15},{... | collective-permute-start | bytes 1572872 | tf_op jit(solution)/shard_map/ppermute | solution.py:403
  8.4 0.6 %collective-permute-start.2 = (bf16[1024,128]{1,0:T(8,128)(2,1)S(1)}, bf16[1024,128]{1,0:T(8,128)(2,1)S(1)}, u32[]{:S(2)}, u32[]{:S(2)}) collective-permute-start(bf16[1024,128]{1,0:T(8,128)(2,1)S(1)} %get-tuple-element.23.q_ref.two_ref), channel_id=1, source_target_pairs={{0,2},{2,0},{4,6},{6,4},{8,10},{10,8},{12,14},{14,12},{1,3},{3,1},... | collective-permute-start | bytes 786440 | tf_op jit(solution)/shard_map/ppermute | solution.py:387
  8.9 0.5 %lists.1.table_ref = s32[40,128]{1,0:T(8,128)S(1)} custom-call(s32[128,128]{1,0:T(8,128)S(1)} %copy-done), custom_call_target="tpu_custom_call" | custom-call | flops 1000 | bytes 100000 | tf_op jit(solution)/shard_map/lists/pallas_call | solution.py:143
  9.5 0.0 collective-permute-done.3.refs_1_
  9.5 3.5 %attend0.1 = (bf16[2048,128]{1,0:T(8,128)(2,1)S(1)}, bf16[2048,128]{1,0:T(8,128)(2,1)S(1)}, f32[1024,128]{1,0:T(8,128)S(1)}, f32[16,128]{1,0:T(8,128)S(1)}) custom-call(s32[40,128]{1,0:T(8,128)S(1)} %lists.1.table_ref, bf16[1024,128]{1,0:T(8,128)(2,1)S(1)} %get-tuple-element.23.q_ref.two_ref, bf16[2,1024,128]{2,1,0:T(8,128)(2,1)S(1)} %get-tuple-element.24.refs_0_, ...), custom_call_target="tpu_custom_call" | custom-call | flops 1048576 | bytes 65536 | tf_op jit(solution)/shard_map/attend0/pallas_call | solution.py:288
  13.0 2.3 %collective-permute-done.2.q_ref.one_ref = bf16[1024,128]{1,0:T(8,128)(2,1)S(1)} collective-permute-done((bf16[1024,128]{1,0:T(8,128)(2,1)S(1)}, bf16[1024,128]{1,0:T(8,128)(2,1)S(1)}, u32[]{:S(2)}, u32[]{:S(2)}) %collective-permute-start.2) | collective-permute-done | bytes 262176 | tf_op jit(solution)/shard_map/ppermute | solution.py:387
  15.3 1.6 %attend1.1 = (f32[1024,128]{1,0:T(8,128)S(1)}, f32[16,128]{1,0:T(8,128)S(1)}) custom-call(s32[40,128]{1,0:T(8,128)S(1)} %lists.1.table_ref, bf16[1024,128]{1,0:T(8,128)(2,1)S(1)} %collective-permute-done.2.q_ref.one_ref, bf16[2048,128]{1,0:T(8,128)(2,1)S(1)} %get-tuple-element.25.refs_0_, bf16[2048,128]{1,0:T(8,128)(2,1)S(1)} %get-tuple-element.26.refs_1_), custom_call_target="tpu_custom_call" | custom-call | flops 1048576 | bytes 65536 | tf_op jit(solution)/shard_map/attend1/pallas_call | solution.py:288
  16.9 0.7 %collective-permute-done.1.refs_2_ = bf16[2,1024,128]{2,1,0:T(8,128)(2,1)S(1)} collective-permute-done((bf16[2,1024,128]{2,1,0:T(8,128)(2,1)S(1)}, bf16[2,1024,128]{2,1,0:T(8,128)(2,1)S(1)}, u32[]{:S(2)}, u32[]{:S(2)}) %collective-permute-start.1) | collective-permute-done | bytes 524320 | tf_op jit(solution)/shard_map/ppermute | solution.py:403
  17.6 0.3 collective-permute-start.4
  17.9 0.2 collective-permute-start.5
  18.1 1.3 %collective-permute-start.7 = (bf16[1024,128]{1,0:T(8,128)(2,1)S(1)}, bf16[1024,128]{1,0:T(8,128)(2,1)S(1)}, u32[]{:S(2)}, u32[]{:S(2)}) collective-permute-start(bf16[1024,128]{1,0:T(8,128)(2,1)S(1)} %choose.1), channel_id=1, source_target_pairs={{0,4},{3,5},{4,8},{7,9},{9,7},{10,6},{13,11},{14,10},{16,20},{19,2... | collective-permute-start | bytes 786440 | tf_op jit(solution)/shard_map/ppermute | solution.py:414
  19.4 0.1 collective-permute-done.4.refs_1_
  19.5 0.7 %collective-permute-done.5.refs_3_ = bf16[2,1024,128]{2,1,0:T(8,128)(2,1)S(1)} collective-permute-done((bf16[2,1024,128]{2,1,0:T(8,128)(2,1)S(1)}, bf16[2,1024,128]{2,1,0:T(8,128)(2,1)S(1)}, u32[]{:S(2)}, u32[]{:S(2)}) %collective-permute-start.5) | collective-permute-done | bytes 524320 | tf_op jit(solution)/shard_map/ppermute | solution.py:393
  20.2 2.9 %attend2.1 = (bf16[1104,128]{1,0:T(8,128)(2,1)S(1)}, bf16[4096,128]{1,0:T(8,128)(2,1)S(1)}, bf16[4096,128]{1,0:T(8,128)(2,1)S(1)}, f32[1024,128]{1,0:T(8,128)S(1)}, f32[16,128]{1,0:T(8,128)S(1)}) custom-call(s32[40,128]{1,0:T(8,128)S(1)} %lists.1.table_ref, ...), custom_call_target="tpu_custom_call", output_to_operand_aliasing={{3}: (6, {}), {4}: (7, {})} | custom-call | flops 1048576 | bytes 65536 | tf_op jit(solution)/shard_map/attend2/pallas_call | solution.py:288
  23.2 0.9 %collective-permute-start.6 = (bf16[1104,128]{1,0:T(8,128)(2,1)S(1)}, bf16[1104,128]{1,0:T(8,128)(2,1)S(1)}, u32[]{:S(2)}, u32[]{:S(2)}) collective-permute-start(bf16[1104,128]{1,0:T(8,128)(2,1)S(1)} %get-tuple-element.40), channel_id=1, source_target_pairs={{0,2},{2,0},{4,6},{6,4},{8,10},{10,8},{12,14},{14,12},{1,3},{3,1},... | collective-permute-start | bytes 847880 | tf_op jit(solution)/shard_map/ppermute | solution.py:387
  24.1 2.3 %collective-permute-done.7.q_ref = bf16[1024,128]{1,0:T(8,128)(2,1)S(1)} collective-permute-done((bf16[1024,128]{1,0:T(8,128)(2,1)S(1)}, bf16[1024,128]{1,0:T(8,128)(2,1)S(1)}, u32[]{:S(2)}, u32[]{:S(2)}) %collective-permute-start.7) | collective-permute-done | bytes 262176 | tf_op jit(solution)/shard_map/ppermute | solution.py:414
  26.4 1.6 %attend4.1 = bf16[1072,128]{1,0:T(8,128)(2,1)S(1)} custom-call(s32[40,128]{1,0:T(8,128)S(1)} %lists.1.table_ref, bf16[1024,128]{1,0:T(8,128)(2,1)S(1)} %collective-permute-done.7.q_ref, bf16[4096,128]{1,0:T(8,128)(2,1)S(1)} %get-tuple-element.34.refs_0_, bf16[4096,128]{1,0:T(8,128)(2,1)S(1)} %get-tuple-element.35.refs_1_), custom_call_target="tpu_custom_call" | custom-call | flops 1048576 | bytes 65536 | tf_op jit(solution)/shard_map/attend4/pallas_call | solution.py:288
  28.0 3.4 %collective-permute-start.8 = (bf16[1072,128]{1,0:T(8,128)(2,1)S(1)}, bf16[1072,128]{1,0:T(8,128)(2,1)S(1)}, u32[]{:S(2)}, u32[]{:S(2)}) collective-permute-start(bf16[1072,128]{1,0:T(8,128)(2,1)S(1)} %attend4.1), channel_id=1, source_target_pairs={{4,2},{6,8},{8,6},{10,12},{5,3},{7,9},{9,7},{11,13},{20,18},{22,24... | collective-permute-start | bytes 823304 | tf_op jit(solution)/shard_map/ppermute | solution.py:437
  31.4 1.6 %attend3.1 = (f32[1024,128]{1,0:T(8,128)S(1)}, f32[16,128]{1,0:T(8,128)S(1)}) custom-call(s32[40,128]{1,0:T(8,128)S(1)} %lists.1.table_ref, bf16[1024,128]{1,0:T(8,128)(2,1)S(1)} %get-tuple-element.23.q_ref.two_ref, bf16[4096,128]{1,0:T(8,128)(2,1)S(1)} %get-tuple-element.34.refs_0_, ...), custom_call_target="tpu_custom_call", output_to_operand_aliasing={{0}: (4, {}), {1}: (5, {})} | custom-call | flops 1048576 | bytes 65536 | tf_op jit(solution)/shard_map/attend3/pallas_call | solution.py:288
  33.0 6.4 %collective-permute-done.8.refs_1_ = bf16[1072,128]{1,0:T(8,128)(2,1)S(1)} collective-permute-done((bf16[1072,128]{1,0:T(8,128)(2,1)S(1)}, bf16[1072,128]{1,0:T(8,128)(2,1)S(1)}, u32[]{:S(2)}, u32[]{:S(2)}) %collective-permute-start.8) | collective-permute-done | bytes 274464 | tf_op jit(solution)/shard_map/ppermute | solution.py:437
  39.4 0.9 %merge.1 = bf16[1024,128]{1,0:T(8,128)(2,1)} custom-call(f32[1024,128]{1,0:T(8,128)S(1)} %get-tuple-element.38.sum_ref, f32[16,128]{1,0:T(8,128)S(1)} %get-tuple-element.39.stat_ref, bf16[1104,128]{1,0:T(8,128)(2,1)S(1)} %collective-permute-done.6.refs_0_, bf16[1072,128]{1,0:T(8,128)(2,1)S(1)} %collective-permute-done.8.refs_1_), custom_call_target="tpu_custom_call" | custom-call | flops 1048576 | bytes 1310720 | tf_op jit(solution)/shard_map/merge/pallas_call | solution.py:360
  (5 shorter events, 0.0 us)
Async XLA Ops:
  0.0 8.9 %copy-start = (s32[128,128]{1,0:T(8,128)S(1)}, s32[128,128]{1,0:T(8,128)}, u32[]{:S(2)}) copy-start(s32[128,128]{1,0:T(8,128)} %allowed_ref.1) | copy-start | bytes 196612
  1.3 8.2 %collective-permute-start.3 = (bf16[2,1024,128]{2,1,0:T(8,128)(2,1)S(1)}, bf16[2,1024,128]{2,1,0:T(8,128)(2,1)S(1)}, u32[]{:S(2)}, u32[]{:S(2)}) collective-permute-start(bf16[2,1024,128]{2,1,0:T(8,128)(2,1)S(1)} %get-tuple-element.24.refs_0_), channel_id=1, source_target_pairs={{0,1},{1,0},{2,3},{3,2},{4,5},{5,4},{6,7},{7,6},{8,9},{9,8},{10,11... | collective-permute-start | bytes 1572872 | tf_op jit(solution)/shard_map/ppermute | solution.py:393
  1.4 15.5 %collective-permute-start = (bf16[2,1024,128]{2,1,0:T(8,128)(2,1)S(1)}, bf16[2,1024,128]{2,1,0:T(8,128)(2,1)S(1)}, u32[]{:S(2)}, u32[]{:S(2)}) collective-permute-start(bf16[2,1024,128]{2,1,0:T(8,128)(2,1)S(1)} %get-tuple-element.24.refs_0_), channel_id=1, source_target_pairs={{0,4},{2,6},{4,0},{5,9},{6,2},{7,11},{8,12},{9,5},{10,14},{11,7},{... | collective-permute-start | bytes 1572872 | tf_op jit(solution)/shard_map/ppermute | solution.py:403
  3.7 13.8 %collective-permute-start.1 = (bf16[2,1024,128]{2,1,0:T(8,128)(2,1)S(1)}, bf16[2,1024,128]{2,1,0:T(8,128)(2,1)S(1)}, u32[]{:S(2)}, u32[]{:S(2)}) collective-permute-start(bf16[2,1024,128]{2,1,0:T(8,128)(2,1)S(1)} %get-tuple-element.24.refs_0_), channel_id=1, source_target_pairs={{1,5},{3,7},{4,8},{5,1},{6,10},{7,3},{8,4},{9,13},{10,6},{11,15},{... | collective-permute-start | bytes 1572872 | tf_op jit(solution)/shard_map/ppermute | solution.py:403
  8.4 6.9 %collective-permute-start.2 = (bf16[1024,128]{1,0:T(8,128)(2,1)S(1)}, bf16[1024,128]{1,0:T(8,128)(2,1)S(1)}, u32[]{:S(2)}, u32[]{:S(2)}) collective-permute-start(bf16[1024,128]{1,0:T(8,128)(2,1)S(1)} %get-tuple-element.23.q_ref.two_ref), channel_id=1, source_target_pairs={{0,2},{2,0},{4,6},{6,4},{8,10},{10,8},{12,14},{14,12},{1,3},{3,1},... | collective-permute-start | bytes 786440 | tf_op jit(solution)/shard_map/ppermute | solution.py:387
  17.6 1.9 %collective-permute-start.4 = (bf16[2,1024,128]{2,1,0:T(8,128)(2,1)S(1)}, bf16[2,1024,128]{2,1,0:T(8,128)(2,1)S(1)}, u32[]{:S(2)}, u32[]{:S(2)}) collective-permute-start(bf16[2,1024,128]{2,1,0:T(8,128)(2,1)S(1)} %collective-permute-done.refs_0_), channel_id=1, source_target_pairs={{0,1},{1,0},{2,3},{3,2},{4,5},{5,4},{6,7},{7,6},{8,9},{9,8},{10,11... | collective-permute-start | bytes 1572872 | tf_op jit(solution)/shard_map/ppermute | solution.py:393
  17.9 2.4 %collective-permute-start.5 = (bf16[2,1024,128]{2,1,0:T(8,128)(2,1)S(1)}, bf16[2,1024,128]{2,1,0:T(8,128)(2,1)S(1)}, u32[]{:S(2)}, u32[]{:S(2)}) collective-permute-start(bf16[2,1024,128]{2,1,0:T(8,128)(2,1)S(1)} %collective-permute-done.1.refs_2_), channel_id=1, source_target_pairs={{0,1},{1,0},{2,3},{3,2},{4,5},{5,4},{6,7},{7,6},{8,9},{9,8},{10,11... | collective-permute-start | bytes 1572872 | tf_op jit(solution)/shard_map/ppermute | solution.py:393
  18.1 8.3 %collective-permute-start.7 = (bf16[1024,128]{1,0:T(8,128)(2,1)S(1)}, bf16[1024,128]{1,0:T(8,128)(2,1)S(1)}, u32[]{:S(2)}, u32[]{:S(2)}) collective-permute-start(bf16[1024,128]{1,0:T(8,128)(2,1)S(1)} %choose.1), channel_id=1, source_target_pairs={{0,4},{3,5},{4,8},{7,9},{9,7},{10,6},{13,11},{14,10},{16,20},{19,2... | collective-permute-start | bytes 786440 | tf_op jit(solution)/shard_map/ppermute | solution.py:414
  23.2 16.2 %collective-permute-start.6 = (bf16[1104,128]{1,0:T(8,128)(2,1)S(1)}, bf16[1104,128]{1,0:T(8,128)(2,1)S(1)}, u32[]{:S(2)}, u32[]{:S(2)}) collective-permute-start(bf16[1104,128]{1,0:T(8,128)(2,1)S(1)} %get-tuple-element.40), channel_id=1, source_target_pairs={{0,2},{2,0},{4,6},{6,4},{8,10},{10,8},{12,14},{14,12},{1,3},{3,1},... | collective-permute-start | bytes 847880 | tf_op jit(solution)/shard_map/ppermute | solution.py:387
  28.0 11.4 %collective-permute-start.8 = (bf16[1072,128]{1,0:T(8,128)(2,1)S(1)}, bf16[1072,128]{1,0:T(8,128)(2,1)S(1)}, u32[]{:S(2)}, u32[]{:S(2)}) collective-permute-start(bf16[1072,128]{1,0:T(8,128)(2,1)S(1)} %attend4.1), channel_id=1, source_target_pairs={{4,2},{6,8},{8,6},{10,12},{5,3},{7,9},{9,7},{11,13},{20,18},{22,24... | collective-permute-start | bytes 823304 | tf_op jit(solution)/shard_map/ppermute | solution.py:437

commit v5 on v4

--- a/solution.py
+++ b/solution.py
@@ -14,7 +14,7 @@
 DROP = -3e38
 FACTOR = HEAD ** (-0.5) * math.log2(math.e)
 COUNT_AT = 64
-WIDTHS = (4, 4, 5, 4, 4)
+WIDTHS = (4, 4, 4, 4, 3)
 
 ANY = pl.BlockSpec(memory_space=pl.ANY)
 HBM = pl.BlockSpec(memory_space=pltpu.HBM)

time: 40.5 us -> 40.8 us (level); the launches traced: 40.3 us -> 40.1 us
  waiting for transfers between devices: 12.5 us -> 11 us
  Pallas kernels: 13.9 us -> 15.1 us
    ppermute x1, waiting for transfers between devices: 6.36 us -> 4.64 us  [shards(): two = lax.ppermute(guest_part, 'blk', homeward)]
    pallas_call x5, Pallas kernels: 11.1 us -> 12.3 us  [attend(): pl.pallas_call(functools.partial(attend_kernel, job * own, WIDTHS[job], l...]
  transfers between devices with their start and end apart: 9 -> 9, of which waited for: 6 -> 6; matrix products, arithmetic and copies ran while one was open for 0% -> 0% of each run, Pallas kernels for 29% -> 32%
where the time goes in v5:
time: 40.8 us; the launch traced here: 40.1 us
  Pallas kernels  15.1 us (37%)
  starting transfers between devices  13.9 us (34%)
  waiting for transfers between devices  11 us (27%)
    pallas_call x5, Pallas kernels, attend(): pl.pallas_call(functools.partial(attend_kernel, job * own, WIDTHS[job], l...  12.3 us
    ppermute x2, starting transfers between devices, trade(): return lax.ppermute(value, ('blk', 'node'), pairs)  6.97 us
    ppermute x1, waiting for transfers between devices, shards(): two = lax.ppermute(guest_part, 'blk', homeward)  4.64 us
    ppermute x1, starting transfers between devices, shards(): two = lax.ppermute(guest_part, 'blk', homeward)  3.43 us
    ppermute x1, waiting for transfers between devices, visit(): return lax.ppermute(value, ('blk', 'node'), pairs)  2.49 us
    ppermute x2, waiting for transfers between devices, hop(): return lax.ppermute(value, 'blk', pairs)  2.31 us
    ppermute x2, starting transfers between devices, hop(): return lax.ppermute(value, 'blk', pairs)  1.62 us
    ppermute x1, starting transfers between devices, visit(): return lax.ppermute(value, ('blk', 'node'), pairs)  1.29 us
  transfers between devices with their start and end apart: 9, of which 6 were waited for; matrix products, arithmetic and copies ran while one was open for 0% of the time, Pallas kernels for 32%

profile of v5, /device:TPU:12, one launch (start us, length us, event | category | flops | bytes accessed | tf_op | source)
XLA Modules:
  0.0 40.1 jit_solution(8397357252760483356)
XLA Ops:
  0.0 1.3 %bundle.1 = (bf16[2,1024,128]{2,1,0:T(8,128)(2,1)S(1)}, bf16[1024,128]{1,0:T(8,128)(2,1)S(1)}) custom-call(bf16[1024,128]{1,0:T(8,128)(2,1)} %q_ref.1, bf16[1024,128]{1,0:T(8,128)(2,1)} %k_ref.1, bf16[1024,128]{1,0:T(8,128)(2,1)} %v_ref.1), custom_call_target="tpu_custom_call" | custom-call | bytes 1048576 | tf_op jit(solution)/shard_map/bundle/pallas_call | solution.py:55
  1.3 0.1 collective-permute-start.3
  1.4 2.4 %collective-permute-start = (bf16[2,1024,128]{2,1,0:T(8,128)(2,1)S(1)}, bf16[2,1024,128]{2,1,0:T(8,128)(2,1)S(1)}, u32[]{:S(2)}, u32[]{:S(2)}) collective-permute-start(bf16[2,1024,128]{2,1,0:T(8,128)(2,1)S(1)} %get-tuple-element.24.refs_0_), channel_id=1, source_target_pairs={{0,4},{2,6},{4,0},{5,9},{6,2},{7,11},{8,12},{9,5},{10,14},{11,7},{... | collective-permute-start | bytes 1572872 | tf_op jit(solution)/shard_map/ppermute | solution.py:403
  3.7 4.6 %collective-permute-start.1 = (bf16[2,1024,128]{2,1,0:T(8,128)(2,1)S(1)}, bf16[2,1024,128]{2,1,0:T(8,128)(2,1)S(1)}, u32[]{:S(2)}, u32[]{:S(2)}) collective-permute-start(bf16[2,1024,128]{2,1,0:T(8,128)(2,1)S(1)} %get-tuple-element.24.refs_0_), channel_id=1, source_target_pairs={{1,5},{3,7},{4,8},{5,1},{6,10},{7,3},{8,4},{9,13},{10,6},{11,15},{... | collective-permute-start | bytes 1572872 | tf_op jit(solution)/shard_map/ppermute | solution.py:403
  8.4 0.6 %collective-permute-start.2 = (bf16[1024,128]{1,0:T(8,128)(2,1)S(1)}, bf16[1024,128]{1,0:T(8,128)(2,1)S(1)}, u32[]{:S(2)}, u32[]{:S(2)}) collective-permute-start(bf16[1024,128]{1,0:T(8,128)(2,1)S(1)} %get-tuple-element.23.q_ref.two_ref), channel_id=1, source_target_pairs={{0,2},{2,0},{4,6},{6,4},{8,10},{10,8},{12,14},{14,12},{1,3},{3,1},... | collective-permute-start | bytes 786440 | tf_op jit(solution)/shard_map/ppermute | solution.py:387
  8.9 0.5 %lists.1.table_ref = s32[40,128]{1,0:T(8,128)S(1)} custom-call(s32[128,128]{1,0:T(8,128)S(1)} %copy-done), custom_call_target="tpu_custom_call" | custom-call | flops 1000 | bytes 100000 | tf_op jit(solution)/shard_map/lists/pallas_call | solution.py:143
  9.5 3.5 %attend0.1 = (bf16[2048,128]{1,0:T(8,128)(2,1)S(1)}, bf16[2048,128]{1,0:T(8,128)(2,1)S(1)}, f32[1024,128]{1,0:T(8,128)S(1)}, f32[16,128]{1,0:T(8,128)S(1)}) custom-call(s32[40,128]{1,0:T(8,128)S(1)} %lists.1.table_ref, bf16[1024,128]{1,0:T(8,128)(2,1)S(1)} %get-tuple-element.23.q_ref.two_ref, bf16[2,1024,128]{2,1,0:T(8,128)(2,1)S(1)} %get-tuple-element.24.refs_0_, ...), custom_call_target="tpu_custom_call" | custom-call | flops 1048576 | bytes 65536 | tf_op jit(solution)/shard_map/attend0/pallas_call | solution.py:288
  13.0 2.3 %collective-permute-done.2.q_ref.one_ref = bf16[1024,128]{1,0:T(8,128)(2,1)S(1)} collective-permute-done((bf16[1024,128]{1,0:T(8,128)(2,1)S(1)}, bf16[1024,128]{1,0:T(8,128)(2,1)S(1)}, u32[]{:S(2)}, u32[]{:S(2)}) %collective-permute-start.2) | collective-permute-done | bytes 262176 | tf_op jit(solution)/shard_map/ppermute | solution.py:387
  15.3 1.6 %attend1.1 = (f32[1024,128]{1,0:T(8,128)S(1)}, f32[16,128]{1,0:T(8,128)S(1)}) custom-call(s32[40,128]{1,0:T(8,128)S(1)} %lists.1.table_ref, bf16[1024,128]{1,0:T(8,128)(2,1)S(1)} %collective-permute-done.2.q_ref.one_ref, bf16[2048,128]{1,0:T(8,128)(2,1)S(1)} %get-tuple-element.25.refs_0_, bf16[2048,128]{1,0:T(8,128)(2,1)S(1)} %get-tuple-element.26.refs_1_), custom_call_target="tpu_custom_call" | custom-call | flops 1048576 | bytes 65536 | tf_op jit(solution)/shard_map/attend1/pallas_call | solution.py:288
  16.9 0.0 collective-permute-done.refs_0_
  16.9 0.7 %collective-permute-done.1.refs_2_ = bf16[2,1024,128]{2,1,0:T(8,128)(2,1)S(1)} collective-permute-done((bf16[2,1024,128]{2,1,0:T(8,128)(2,1)S(1)}, bf16[2,1024,128]{2,1,0:T(8,128)(2,1)S(1)}, u32[]{:S(2)}, u32[]{:S(2)}) %collective-permute-start.1) | collective-permute-done | bytes 524320 | tf_op jit(solution)/shard_map/ppermute | solution.py:403
  17.6 0.3 collective-permute-start.4
  17.9 0.2 collective-permute-start.5
  18.1 1.3 %collective-permute-start.7 = (bf16[1024,128]{1,0:T(8,128)(2,1)S(1)}, bf16[1024,128]{1,0:T(8,128)(2,1)S(1)}, u32[]{:S(2)}, u32[]{:S(2)}) collective-permute-start(bf16[1024,128]{1,0:T(8,128)(2,1)S(1)} %choose.1), channel_id=1, source_target_pairs={{0,4},{3,5},{4,8},{7,9},{9,7},{10,6},{13,11},{14,10},{16,20},{19,2... | collective-permute-start | bytes 786440 | tf_op jit(solution)/shard_map/ppermute | solution.py:414
  19.4 0.1 collective-permute-done.4.refs_1_
  19.5 0.7 %collective-permute-done.5.refs_3_ = bf16[2,1024,128]{2,1,0:T(8,128)(2,1)S(1)} collective-permute-done((bf16[2,1024,128]{2,1,0:T(8,128)(2,1)S(1)}, bf16[2,1024,128]{2,1,0:T(8,128)(2,1)S(1)}, u32[]{:S(2)}, u32[]{:S(2)}) %collective-permute-start.5) | collective-permute-done | bytes 524320 | tf_op jit(solution)/shard_map/ppermute | solution.py:393
  20.2 2.6 %attend2.1 = (bf16[1104,128]{1,0:T(8,128)(2,1)S(1)}, bf16[4096,128]{1,0:T(8,128)(2,1)S(1)}, bf16[4096,128]{1,0:T(8,128)(2,1)S(1)}, f32[1024,128]{1,0:T(8,128)S(1)}, f32[16,128]{1,0:T(8,128)S(1)}) custom-call(s32[40,128]{1,0:T(8,128)S(1)} %lists.1.table_ref, ...), custom_call_target="tpu_custom_call", output_to_operand_aliasing={{3}: (6, {}), {4}: (7, {})} | custom-call | flops 1048576 | bytes 65536 | tf_op jit(solution)/shard_map/attend2/pallas_call | solution.py:288
  22.9 1.0 %collective-permute-start.6 = (bf16[1104,128]{1,0:T(8,128)(2,1)S(1)}, bf16[1104,128]{1,0:T(8,128)(2,1)S(1)}, u32[]{:S(2)}, u32[]{:S(2)}) collective-permute-start(bf16[1104,128]{1,0:T(8,128)(2,1)S(1)} %get-tuple-element.40), channel_id=1, source_target_pairs={{0,2},{2,0},{4,6},{6,4},{8,10},{10,8},{12,14},{14,12},{1,3},{3,1},... | collective-permute-start | bytes 847880 | tf_op jit(solution)/shard_map/ppermute | solution.py:387
  23.9 2.5 %collective-permute-done.7.q_ref = bf16[1024,128]{1,0:T(8,128)(2,1)S(1)} collective-permute-done((bf16[1024,128]{1,0:T(8,128)(2,1)S(1)}, bf16[1024,128]{1,0:T(8,128)(2,1)S(1)}, u32[]{:S(2)}, u32[]{:S(2)}) %collective-permute-start.7) | collective-permute-done | bytes 262176 | tf_op jit(solution)/shard_map/ppermute | solution.py:414
  26.4 2.2 %attend4.1 = bf16[1072,128]{1,0:T(8,128)(2,1)S(1)} custom-call(s32[40,128]{1,0:T(8,128)S(1)} %lists.1.table_ref, bf16[1024,128]{1,0:T(8,128)(2,1)S(1)} %collective-permute-done.7.q_ref, bf16[4096,128]{1,0:T(8,128)(2,1)S(1)} %get-tuple-element.34.refs_0_, bf16[4096,128]{1,0:T(8,128)(2,1)S(1)} %get-tuple-element.35.refs_1_), custom_call_target="tpu_custom_call" | custom-call | flops 1048576 | bytes 65536 | tf_op jit(solution)/shard_map/attend4/pallas_call | solution.py:288
  28.6 3.4 %collective-permute-start.8 = (bf16[1072,128]{1,0:T(8,128)(2,1)S(1)}, bf16[1072,128]{1,0:T(8,128)(2,1)S(1)}, u32[]{:S(2)}, u32[]{:S(2)}) collective-permute-start(bf16[1072,128]{1,0:T(8,128)(2,1)S(1)} %attend4.1), channel_id=1, source_target_pairs={{4,2},{6,8},{8,6},{10,12},{5,3},{7,9},{9,7},{11,13},{20,18},{22,24... | collective-permute-start | bytes 823304 | tf_op jit(solution)/shard_map/ppermute | solution.py:437
  32.1 2.5 %attend3.1 = (f32[1024,128]{1,0:T(8,128)S(1)}, f32[16,128]{1,0:T(8,128)S(1)}) custom-call(s32[40,128]{1,0:T(8,128)S(1)} %lists.1.table_ref, bf16[1024,128]{1,0:T(8,128)(2,1)S(1)} %get-tuple-element.23.q_ref.two_ref, bf16[4096,128]{1,0:T(8,128)(2,1)S(1)} %get-tuple-element.34.refs_0_, ...), custom_call_target="tpu_custom_call", output_to_operand_aliasing={{0}: (4, {}), {1}: (5, {})} | custom-call | flops 1048576 | bytes 65536 | tf_op jit(solution)/shard_map/attend3/pallas_call | solution.py:288
  34.5 4.6 %collective-permute-done.8.refs_1_ = bf16[1072,128]{1,0:T(8,128)(2,1)S(1)} collective-permute-done((bf16[1072,128]{1,0:T(8,128)(2,1)S(1)}, bf16[1072,128]{1,0:T(8,128)(2,1)S(1)}, u32[]{:S(2)}, u32[]{:S(2)}) %collective-permute-start.8) | collective-permute-done | bytes 274464 | tf_op jit(solution)/shard_map/ppermute | solution.py:437
  39.2 0.9 %merge.1 = bf16[1024,128]{1,0:T(8,128)(2,1)} custom-call(f32[1024,128]{1,0:T(8,128)S(1)} %get-tuple-element.38.sum_ref, f32[16,128]{1,0:T(8,128)S(1)} %get-tuple-element.39.stat_ref, bf16[1104,128]{1,0:T(8,128)(2,1)S(1)} %collective-permute-done.6.refs_0_, bf16[1072,128]{1,0:T(8,128)(2,1)S(1)} %collective-permute-done.8.refs_1_), custom_call_target="tpu_custom_call" | custom-call | flops 1048576 | bytes 1310720 | tf_op jit(solution)/shard_map/merge/pallas_call | solution.py:360
  (5 shorter events, 0.0 us)
Async XLA Ops:
  0.0 8.9 %copy-start = (s32[128,128]{1,0:T(8,128)S(1)}, s32[128,128]{1,0:T(8,128)}, u32[]{:S(2)}) copy-start(s32[128,128]{1,0:T(8,128)} %allowed_ref.1) | copy-start | bytes 196612
  1.3 8.2 %collective-permute-start.3 = (bf16[2,1024,128]{2,1,0:T(8,128)(2,1)S(1)}, bf16[2,1024,128]{2,1,0:T(8,128)(2,1)S(1)}, u32[]{:S(2)}, u32[]{:S(2)}) collective-permute-start(bf16[2,1024,128]{2,1,0:T(8,128)(2,1)S(1)} %get-tuple-element.24.refs_0_), channel_id=1, source_target_pairs={{0,1},{1,0},{2,3},{3,2},{4,5},{5,4},{6,7},{7,6},{8,9},{9,8},{10,11... | collective-permute-start | bytes 1572872 | tf_op jit(solution)/shard_map/ppermute | solution.py:393
  1.4 15.5 %collective-permute-start = (bf16[2,1024,128]{2,1,0:T(8,128)(2,1)S(1)}, bf16[2,1024,128]{2,1,0:T(8,128)(2,1)S(1)}, u32[]{:S(2)}, u32[]{:S(2)}) collective-permute-start(bf16[2,1024,128]{2,1,0:T(8,128)(2,1)S(1)} %get-tuple-element.24.refs_0_), channel_id=1, source_target_pairs={{0,4},{2,6},{4,0},{5,9},{6,2},{7,11},{8,12},{9,5},{10,14},{11,7},{... | collective-permute-start | bytes 1572872 | tf_op jit(solution)/shard_map/ppermute | solution.py:403
  3.7 13.8 %collective-permute-start.1 = (bf16[2,1024,128]{2,1,0:T(8,128)(2,1)S(1)}, bf16[2,1024,128]{2,1,0:T(8,128)(2,1)S(1)}, u32[]{:S(2)}, u32[]{:S(2)}) collective-permute-start(bf16[2,1024,128]{2,1,0:T(8,128)(2,1)S(1)} %get-tuple-element.24.refs_0_), channel_id=1, source_target_pairs={{1,5},{3,7},{4,8},{5,1},{6,10},{7,3},{8,4},{9,13},{10,6},{11,15},{... | collective-permute-start | bytes 1572872 | tf_op jit(solution)/shard_map/ppermute | solution.py:403
  8.4 6.9 %collective-permute-start.2 = (bf16[1024,128]{1,0:T(8,128)(2,1)S(1)}, bf16[1024,128]{1,0:T(8,128)(2,1)S(1)}, u32[]{:S(2)}, u32[]{:S(2)}) collective-permute-start(bf16[1024,128]{1,0:T(8,128)(2,1)S(1)} %get-tuple-element.23.q_ref.two_ref), channel_id=1, source_target_pairs={{0,2},{2,0},{4,6},{6,4},{8,10},{10,8},{12,14},{14,12},{1,3},{3,1},... | collective-permute-start | bytes 786440 | tf_op jit(solution)/shard_map/ppermute | solution.py:387
  17.6 1.9 %collective-permute-start.4 = (bf16[2,1024,128]{2,1,0:T(8,128)(2,1)S(1)}, bf16[2,1024,128]{2,1,0:T(8,128)(2,1)S(1)}, u32[]{:S(2)}, u32[]{:S(2)}) collective-permute-start(bf16[2,1024,128]{2,1,0:T(8,128)(2,1)S(1)} %collective-permute-done.refs_0_), channel_id=1, source_target_pairs={{0,1},{1,0},{2,3},{3,2},{4,5},{5,4},{6,7},{7,6},{8,9},{9,8},{10,11... | collective-permute-start | bytes 1572872 | tf_op jit(solution)/shard_map/ppermute | solution.py:393
  17.9 2.4 %collective-permute-start.5 = (bf16[2,1024,128]{2,1,0:T(8,128)(2,1)S(1)}, bf16[2,1024,128]{2,1,0:T(8,128)(2,1)S(1)}, u32[]{:S(2)}, u32[]{:S(2)}) collective-permute-start(bf16[2,1024,128]{2,1,0:T(8,128)(2,1)S(1)} %collective-permute-done.1.refs_2_), channel_id=1, source_target_pairs={{0,1},{1,0},{2,3},{3,2},{4,5},{5,4},{6,7},{7,6},{8,9},{9,8},{10,11... | collective-permute-start | bytes 1572872 | tf_op jit(solution)/shard_map/ppermute | solution.py:393
  18.1 8.3 %collective-permute-start.7 = (bf16[1024,128]{1,0:T(8,128)(2,1)S(1)}, bf16[1024,128]{1,0:T(8,128)(2,1)S(1)}, u32[]{:S(2)}, u32[]{:S(2)}) collective-permute-start(bf16[1024,128]{1,0:T(8,128)(2,1)S(1)} %choose.1), channel_id=1, source_target_pairs={{0,4},{3,5},{4,8},{7,9},{9,7},{10,6},{13,11},{14,10},{16,20},{19,2... | collective-permute-start | bytes 786440 | tf_op jit(solution)/shard_map/ppermute | solution.py:414
  22.9 16.3 %collective-permute-start.6 = (bf16[1104,128]{1,0:T(8,128)(2,1)S(1)}, bf16[1104,128]{1,0:T(8,128)(2,1)S(1)}, u32[]{:S(2)}, u32[]{:S(2)}) collective-permute-start(bf16[1104,128]{1,0:T(8,128)(2,1)S(1)} %get-tuple-element.40), channel_id=1, source_target_pairs={{0,2},{2,0},{4,6},{6,4},{8,10},{10,8},{12,14},{14,12},{1,3},{3,1},... | collective-permute-start | bytes 847880 | tf_op jit(solution)/shard_map/ppermute | solution.py:387
  28.6 10.6 %collective-permute-start.8 = (bf16[1072,128]{1,0:T(8,128)(2,1)S(1)}, bf16[1072,128]{1,0:T(8,128)(2,1)S(1)}, u32[]{:S(2)}, u32[]{:S(2)}) collective-permute-start(bf16[1072,128]{1,0:T(8,128)(2,1)S(1)} %attend4.1), channel_id=1, source_target_pairs={{4,2},{6,8},{8,6},{10,12},{5,3},{7,9},{9,7},{11,13},{20,18},{22,24... | collective-permute-start | bytes 823304 | tf_op jit(solution)/shard_map/ppermute | solution.py:437
